TPU v7x, 32 devices: a whole 2x2x4 slice. The times are simulated.
32 devices in a mesh: dp: 4 (over y, core), seq: 8 (over z, x).
Axes of the slice: x: 2, y: 2, z: 4, core: 2. Of those that a mesh axis runs over, the one named last changes fastest.
Arguments:
- tokens: bfloat16 [4, 2048, 2048], P('dp', 'seq'), may hold values from -6 to 6
- segment_ids: int32 [4, 2048], P('dp'), may hold values from 0 to 2, as said below
- ln1_gain: bfloat16 [2048], P('dp'), may hold values from 0.5 to 1.5
- ln1_bias: bfloat16 [2048], P('dp'), may hold values from -1.5 to 1.5
- w_qkv: bfloat16 [2048, 6144], P(('dp', 'seq')), may hold values from -0.1875 to 0.1875
- b_qkv: bfloat16 [6144], P('dp'), may hold values from -1.5 to 1.5
- w_out: bfloat16 [2048, 2048], P(('dp', 'seq')), may hold values from -0.375 to 0.375
- b_out: bfloat16 [2048], P('dp'), may hold values from -1.5 to 1.5
- ln2_gain: bfloat16 [2048], P('dp'), may hold values from 0.5 to 1.5
- ln2_bias: bfloat16 [2048], P('dp'), may hold values from -1.5 to 1.5
- w_up: bfloat16 [2048, 8192], P('dp', 'seq'), may hold values from -0.125 to 0.125
- b_up: bfloat16 [8192], P('seq'), may hold values from -1.5 to 1.5
- w_down: bfloat16 [8192, 2048], P('seq', 'dp'), may hold values from -0.09375 to 0.09375
- b_down: bfloat16 [2048], P('dp'), may hold values from -1.5 to 1.5
- cotangent: bfloat16 [4, 2048, 2048], P('dp', 'seq'), may hold values from -6 to 6
Outputs:
- layer_output: bfloat16 [4, 2048, 2048], P('dp', 'seq')
- input_grad: float32 [4, 2048, 2048], P('dp', 'seq')
- ln1_gain_grad: float32 [2048], replicated
- ln1_bias_grad: float32 [2048], replicated
- w_qkv_grad: float32 [2048, 6144], P(('dp', 'seq'))
- b_qkv_grad: float32 [6144], replicated
- w_out_grad: float32 [2048, 2048], P(('dp', 'seq'))
- b_out_grad: float32 [2048], replicated
- ln2_gain_grad: float32 [2048], replicated
- ln2_bias_grad: float32 [2048], replicated
- w_up_grad: float32 [2048, 8192], P('dp', 'seq')
- b_up_grad: float32 [8192], replicated
- w_down_grad: float32 [8192, 2048], P('seq', 'dp')
- b_down_grad: float32 [2048], replicated
- rms_stats: float32 [3], replicated
Inputs may be any that keep to these rules, and one draw needn't show every extreme that they name: `segment_ids`: each row holds document 1 from position 0, then document 2, then a padding tail of id 0 that is never empty; ids never fall except into the padding.
All inputs are finite; a program needn't handle non-finite values.
Results may differ from a plain program's by a relative error of at most 0.02.
Values may be sent and summed in bfloat16 or wider, within the bound.
No kernel may reach another device: no remote copies, remote signals or barrier semaphores. Data moves between devices by JAX's collectives and lax.ppermute only.
A program may use at most 384 MiB of HBM per device.

v0:
```python
import jax
import jax.numpy as jnp
from jax import lax
from jax.sharding import PartitionSpec as P

HEADS = 16
FF = 8192


EPSILON = 1e-05
NEG_FILL = -1e30


def layer_norm(values, gain_vec, shift_vec):
    average = jnp.mean(values, axis=-1, keepdims=True)
    centered = values - average
    variance = jnp.mean(centered * centered, axis=-1, keepdims=True)
    return centered * lax.rsqrt(variance + EPSILON) * gain_vec + shift_vec


def positions_of(segments):
    length = segments.shape[-1]
    places = jnp.arange(length, dtype=jnp.int32)
    before = jnp.concatenate(
        [jnp.full(segments.shape[:-1] + (1,), -1, jnp.int32), segments[..., :-1]], axis=-1
    )
    starts = lax.cummax(jnp.where(segments != before, places, 0), axis=segments.ndim - 1)
    return places - starts


def rotate(values, positions):
    half_size = values.shape[-1] // 2
    freqs_table = 10000.0 ** (-jnp.arange(half_size, dtype=jnp.float32) / half_size)
    angles = positions.astype(jnp.float32)[..., None, None] * freqs_table
    cosine = jnp.cos(angles)
    sine_part = jnp.sin(angles)
    first_half = values[..., :half_size]
    second_half = values[..., half_size:]
    return jnp.concatenate(
        [
            first_half * cosine - second_half * sine_part,
            second_half * cosine + first_half * sine_part,
        ],
        axis=-1,
    )


def rotate_back(gradient, positions):
    return jax.vjp(lambda inner_value: rotate(inner_value, positions), jnp.zeros_like(gradient))[1](
        gradient
    )[0]


def gelu_back(hidden_pre, act_grad):
    return jax.vjp(lambda inner_value: jax.nn.gelu(inner_value, approximate=True), hidden_pre)[1](
        act_grad
    )[0]


def score_block(query_row, key_row, allowed_row, score_scale):
    scores = (
        jnp.einsum("chd,khd->hck", query_row, key_row, preferred_element_type=jnp.float32)
        * score_scale
    )
    return jax.nn.softmax(jnp.where(allowed_row[None], scores, NEG_FILL), axis=-1)


def attend_rows(queries, keys_all, values_all, allowed, score_scale):

    def one_row(row_item):
        query_row, key_row, value_row, allowed_row = row_item
        weights = score_block(query_row, key_row, allowed_row, score_scale).astype(jnp.bfloat16)
        return jnp.einsum("hck,khd->chd", weights, value_row, preferred_element_type=jnp.float32)

    return lax.map(one_row, (queries, keys_all, values_all, allowed))


def attend_back(queries, keys_all, values_all, allowed, grad_heads, score_scale):

    def one_row(row_item):
        query_row, key_row, value_row, allowed_row, grad_row = row_item
        weights = score_block(query_row, key_row, allowed_row, score_scale)
        weight_grad = jnp.einsum(
            "chd,khd->hck", grad_row, value_row, preferred_element_type=jnp.float32
        )
        score_grad = weights * (
            weight_grad - jnp.sum(weights * weight_grad, axis=-1, keepdims=True)
        )
        score_low = score_grad.astype(jnp.bfloat16)
        query_grad = (
            jnp.einsum("hck,khd->chd", score_low, key_row, preferred_element_type=jnp.float32)
            * score_scale
        )
        key_grad = (
            jnp.einsum("hck,chd->khd", score_low, query_row, preferred_element_type=jnp.float32)
            * score_scale
        )
        value_grad = jnp.einsum(
            "hck,chd->khd",
            weights.astype(jnp.bfloat16),
            grad_row,
            preferred_element_type=jnp.float32,
        )
        return (query_grad, key_grad, value_grad)

    return lax.map(one_row, (queries, keys_all, values_all, allowed, grad_heads))


def local(
    tokens,
    segment_ids,
    ln1_gain,
    ln1_bias,
    w_qkv,
    b_qkv,
    w_out,
    b_out,
    ln2_gain,
    ln2_bias,
    w_up,
    b_up,
    w_down,
    b_down,
    cotangent,
):
    row_count, span_len, model_width = tokens.shape
    head_count = HEADS
    head_size = model_width // head_count
    score_scale = head_size ** (-0.5)
    seq_len = segment_ids.shape[1]
    split_shape = (row_count, span_len, head_count, head_size)
    flat_shape = (row_count, span_len, model_width)
    offset = lax.axis_index("seq") * span_len
    token_order = jnp.arange(seq_len, dtype=jnp.int32)
    local_order = offset + jnp.arange(span_len, dtype=jnp.int32)
    places = lax.dynamic_slice_in_dim(positions_of(segment_ids), offset, span_len, 1)
    local_segments = lax.dynamic_slice_in_dim(segment_ids, offset, span_len, 1)
    allowed = (local_segments[:, :, None] == segment_ids[:, None, :]) & (
        token_order[None, None, :] <= local_order[None, :, None]
    )
    stream = tokens.astype(jnp.float32)
    qkv_rows, out_rows = (
        lax.all_gather(w_qkv, "seq", axis=0, tiled=True),
        lax.all_gather(w_out, "seq", axis=0, tiled=True),
    )
    (
        qkv_weight,
        out_weight,
        up_slice,
        down_slice,
        gain_one,
        shift_one,
        qkv_bias,
        out_bias,
        gain_two,
        shift_two,
        down_bias,
    ) = (
        lax.all_gather(qkv_rows, "dp", axis=0, tiled=True),
        lax.all_gather(out_rows, "dp", axis=0, tiled=True),
        lax.all_gather(w_up, "dp", axis=0, tiled=True),
        lax.all_gather(w_down, "dp", axis=1, tiled=True),
        lax.all_gather(ln1_gain, "dp", axis=0, tiled=True),
        lax.all_gather(ln1_bias, "dp", axis=0, tiled=True),
        lax.all_gather(b_qkv, "dp", axis=0, tiled=True),
        lax.all_gather(b_out, "dp", axis=0, tiled=True),
        lax.all_gather(ln2_gain, "dp", axis=0, tiled=True),
        lax.all_gather(ln2_bias, "dp", axis=0, tiled=True),
        lax.all_gather(b_down, "dp", axis=0, tiled=True),
    )
    gain_one = gain_one.astype(jnp.float32)
    shift_one = shift_one.astype(jnp.float32)
    gain_two = gain_two.astype(jnp.float32)
    shift_two = shift_two.astype(jnp.float32)
    normed_one = layer_norm(stream, gain_one, shift_one).astype(jnp.bfloat16)
    projected = jnp.einsum(
        "rcd,de->rce", normed_one, qkv_weight, preferred_element_type=jnp.float32
    ) + qkv_bias.astype(jnp.float32)
    queries = rotate(projected[..., :model_width].reshape(split_shape), places).astype(jnp.bfloat16)
    keys_mine = rotate(
        projected[..., model_width : 2 * model_width].reshape(split_shape), places
    ).astype(jnp.bfloat16)
    values_mine = projected[..., 2 * model_width :].reshape(split_shape).astype(jnp.bfloat16)
    keys_all, values_all = (
        lax.all_gather(keys_mine, "seq", axis=1, tiled=True),
        lax.all_gather(values_mine, "seq", axis=1, tiled=True),
    )
    mixed_heads = attend_rows(queries, keys_all, values_all, allowed, score_scale)
    attended = mixed_heads.reshape(flat_shape).astype(jnp.bfloat16)
    attn_branch = jnp.einsum(
        "rcd,de->rce", attended, out_weight, preferred_element_type=jnp.float32
    ) + out_bias.astype(jnp.float32)
    middle = stream + attn_branch
    normed_two = layer_norm(middle, gain_two, shift_two).astype(jnp.bfloat16)
    normed_full = lax.all_gather(normed_two, "seq", axis=1, tiled=True)
    hidden_pre = jnp.einsum(
        "rld,df->rlf", normed_full, up_slice, preferred_element_type=jnp.float32
    ) + b_up.astype(jnp.float32)
    activated = jax.nn.gelu(hidden_pre, approximate=True).astype(jnp.bfloat16)
    partial_out = jnp.einsum(
        "rlf,fd->rld", activated, down_slice, preferred_element_type=jnp.float32
    )
    mlp_branch = lax.psum_scatter(
        partial_out.astype(jnp.bfloat16), "seq", scatter_dimension=1, tiled=True
    ).astype(jnp.float32) + down_bias.astype(jnp.float32)
    output = middle + mlp_branch
    valid_rows = (local_segments != 0)[..., None]
    square_sums = jnp.stack(
        [
            jnp.sum(jnp.where(valid_rows, output * output, 0.0)),
            jnp.sum(jnp.where(valid_rows, attn_branch * attn_branch, 0.0)),
            jnp.sum(jnp.where(valid_rows, mlp_branch * mlp_branch, 0.0)),
        ]
    )
    counted = jnp.sum((local_segments != 0).astype(jnp.float32))
    out_grad = cotangent.astype(jnp.float32)
    down_bias_grad = jnp.sum(out_grad, axis=(0, 1))
    low_full = lax.all_gather(cotangent, "seq", axis=1, tiled=True)
    down_weight_grad = jnp.einsum(
        "rlf,rld->fd", activated, low_full, preferred_element_type=jnp.float32
    )
    act_grad = jnp.einsum("rld,fd->rlf", low_full, down_slice, preferred_element_type=jnp.float32)
    up_low = gelu_back(hidden_pre, act_grad).astype(jnp.bfloat16)
    up_weight_grad = jnp.einsum(
        "rld,rlf->df", normed_full, up_low, preferred_element_type=jnp.float32
    )
    up_part = jnp.sum(up_low.astype(jnp.float32), axis=(0, 1))
    up_bias_grad = lax.dynamic_update_slice(
        jnp.zeros((FF,), jnp.float32), up_part, (lax.axis_index("seq") * up_part.shape[0],)
    )
    normed_terms = jnp.einsum("rlf,df->rld", up_low, up_slice, preferred_element_type=jnp.float32)
    normed_two_grad = lax.psum_scatter(
        normed_terms.astype(jnp.bfloat16), "seq", scatter_dimension=1, tiled=True
    ).astype(jnp.float32)
    up_grad_slice, down_grad_slice = (up_weight_grad, down_weight_grad)
    second_pull = jax.vjp(layer_norm, middle, gain_two, shift_two)[1]
    middle_part, gain_two_grad, shift_two_grad = second_pull(normed_two_grad)
    middle_grad = out_grad + middle_part
    attn_low = middle_grad.astype(jnp.bfloat16)
    out_weight_grad = jnp.einsum(
        "rcd,rce->de", attended, attn_low, preferred_element_type=jnp.float32
    )
    out_bias_grad = jnp.sum(attn_low.astype(jnp.float32), axis=(0, 1))
    attended_grad = jnp.einsum(
        "rce,de->rcd", attn_low, out_weight, preferred_element_type=jnp.float32
    )
    grad_heads = attended_grad.astype(jnp.bfloat16).reshape(split_shape)
    query_grad, key_grad_all, value_grad_all = attend_back(
        queries, keys_all, values_all, allowed, grad_heads, score_scale
    )
    key_grad, value_grad = (
        lax.psum_scatter(
            key_grad_all.astype(jnp.bfloat16), "seq", scatter_dimension=1, tiled=True
        ).astype(jnp.float32),
        lax.psum_scatter(
            value_grad_all.astype(jnp.bfloat16), "seq", scatter_dimension=1, tiled=True
        ).astype(jnp.float32),
    )
    projected_grad = jnp.concatenate(
        [
            rotate_back(query_grad, places).reshape(flat_shape),
            rotate_back(key_grad, places).reshape(flat_shape),
            value_grad.reshape(flat_shape),
        ],
        axis=-1,
    )
    projected_low = projected_grad.astype(jnp.bfloat16)
    qkv_weight_grad = jnp.einsum(
        "rcd,rce->de", normed_one, projected_low, preferred_element_type=jnp.float32
    )
    qkv_bias_grad = jnp.sum(projected_low.astype(jnp.float32), axis=(0, 1))
    normed_one_grad = jnp.einsum(
        "rce,de->rcd", projected_low, qkv_weight, preferred_element_type=jnp.float32
    )
    first_pull = jax.vjp(layer_norm, stream, gain_one, shift_one)[1]
    stream_part, gain_one_grad, shift_one_grad = first_pull(normed_one_grad)
    input_grad = middle_grad + stream_part
    qkv_grad_rows, out_grad_rows, up_grad_out, down_grad_out = (
        lax.psum_scatter(
            qkv_weight_grad.astype(jnp.bfloat16), "dp", scatter_dimension=0, tiled=True
        ).astype(jnp.float32),
        lax.psum_scatter(
            out_weight_grad.astype(jnp.bfloat16), "dp", scatter_dimension=0, tiled=True
        ).astype(jnp.float32),
        lax.psum_scatter(
            up_grad_slice.astype(jnp.bfloat16), "dp", scatter_dimension=0, tiled=True
        ).astype(jnp.float32),
        lax.psum_scatter(
            down_grad_slice.astype(jnp.bfloat16), "dp", scatter_dimension=1, tiled=True
        ).astype(jnp.float32),
    )
    qkv_grad_out, out_grad_out = (
        lax.psum_scatter(
            qkv_grad_rows.astype(jnp.bfloat16), "seq", scatter_dimension=0, tiled=True
        ).astype(jnp.float32),
        lax.psum_scatter(
            out_grad_rows.astype(jnp.bfloat16), "seq", scatter_dimension=0, tiled=True
        ).astype(jnp.float32),
    )
    (
        total_sums,
        total_count,
        gain_one_total,
        shift_one_total,
        qkv_bias_total,
        out_bias_total,
        gain_two_total,
        shift_two_total,
        up_bias_total,
        down_bias_total,
    ) = lax.psum(
        (
            square_sums,
            counted,
            gain_one_grad,
            shift_one_grad,
            qkv_bias_grad,
            out_bias_grad,
            gain_two_grad,
            shift_two_grad,
            up_bias_grad,
            down_bias_grad,
        ),
        ("dp", "seq"),
    )
    rms_stats = jnp.sqrt(total_sums / (total_count * model_width))
    return (
        output.astype(jnp.bfloat16),
        input_grad,
        gain_one_total,
        shift_one_total,
        qkv_grad_out,
        qkv_bias_total,
        out_grad_out,
        out_bias_total,
        gain_two_total,
        shift_two_total,
        up_grad_out,
        up_bias_total,
        down_grad_out,
        down_bias_total,
        rms_stats,
    )


def solution(mesh):
    placed = (
        P("dp", "seq", None),
        P("dp", None),
        P("dp"),
        P("dp"),
        P(("dp", "seq"), None),
        P("dp"),
        P(("dp", "seq"), None),
        P("dp"),
        P("dp"),
        P("dp"),
        P("dp", "seq"),
        P("seq"),
        P("seq", "dp"),
        P("dp"),
        P("dp", "seq", None),
    )
    return jax.shard_map(
        local,
        mesh=mesh,
        in_specs=placed,
        out_specs=(
            P("dp", "seq", None),
            P("dp", "seq", None),
            P(),
            P(),
            P(("dp", "seq"), None),
            P(),
            P(("dp", "seq"), None),
            P(),
            P(),
            P(),
            P("dp", "seq"),
            P(),
            P("seq", "dp"),
            P(),
            P(),
        ),
        check_vma=False,
    )
```

profile of v0, /device:TPU:0, one launch (start us, length us, event | category | flops | bytes accessed | tf_op | source)
XLA Modules:
  0.0 2186.9 jit_solution(13316312522141149452)
XLA Ops:
  8.0 104.0 %all-gather.18.cloned.1.call-done = bf16[512,6144]{1,0:T(8,128)(2,1)} async-done(((bf16[64,6144]{1,0:T(8,128)(2,1)}), bf16[512,6144]{1,0:T(8,128)(2,1)}) %all-gather.18.cloned.1.call-update) | async-done | bytes 6291472 | tf_op jit(solution)/shard_map/all_gather | solution.py:143
  114.4 5.1 all-gather.1
  119.6 5.2 all-gather
  125.5 5.2 all-gather.2
  131.4 135.2 %all-gather.20.cloned.1.call-done = bf16[2048,6144]{1,0:T(8,128)(2,1)} async-done(((bf16[512,6144]{1,0:T(8,128)(2,1)}), bf16[2048,6144]{1,0:T(8,128)(2,1)}) %all-gather.20.cloned.1.call-update) | async-done | bytes 25165840 | tf_op jit(solution)/shard_map/all_gather | solution.py:159
  266.6 11.8 fusion.32
  278.9 2.3 copy-done.16
  283.3 2.7 fusion.70
  286.1 1.6 pad_maximum_fusion.4
  287.8 2.7 slice.54
  290.5 2.3 copy.79
  292.9 25.1 %all-gather.26.cloned.1.call-done = bf16[512,2048]{1,0:T(8,128)(2,1)} async-done(((bf16[64,2048]{1,0:T(8,128)(2,1)}), bf16[512,2048]{1,0:T(8,128)(2,1)}) %all-gather.26.cloned.1.call-update) | async-done | bytes 2097168 | tf_op jit(solution)/shard_map/all_gather | solution.py:144
  319.5 5.6 all-gather.5
  325.1 5.2 all-gather.4
  330.3 5.2 all-gather.3
  337.0 107.0 %all-gather.24.cloned.1.call-done = bf16[1,2048,16,128]{3,1,2,0:T(8,128)(2,1)} async-done(((bf16[1,256,16,128]{3,1,2,0:T(8,128)(2,1)}), bf16[1,2048,16,128]{3,1,2,0:T(8,128)(2,1)}) %all-gather.24.cloned.1.call-update) | async-done | bytes 8388624 | tf_op jit(solution)/shard_map/all_gather | solution.py:185
  444.1 17.5 fusion.23
  461.5 38.2 %fusion.93 = (f32[16,256]{1,0:T(8,128)S(1)}, f32[16,256,2048]{2,1,0:T(8,128)}) fusion(f32[16,256,2048]{2,1,0:T(8,128)} %fusion.23, pred[256,2048]{1,0:T(8,128)(4,1)} %fusion.57), kind=kOutput, calls=%fused_computation.153 | output fusion | flops 50333696 | bytes 67649536 | tf_op jit(solution)/shard_map/while/body/eval_jaxpr/sub | solution.py:65
  499.7 70.4 %all-gather.22.cloned.1.call-done = bf16[1,2048,16,128]{1,3,2,0:T(8,128)(2,1)} async-done(((bf16[1,256,16,128]{1,3,2,0:T(8,128)(2,1)}), bf16[1,2048,16,128]{1,3,2,0:T(8,128)(2,1)}) %all-gather.22.cloned.1.call-update) | async-done | bytes 8388624 | tf_op jit(solution)/shard_map/all_gather | solution.py:186
  570.1 19.7 fusion.60
  589.8 38.2 %all-gather.28.cloned.1.call-done = bf16[2048,2048]{1,0:T(8,128)(2,1)} async-done(((bf16[512,2048]{1,0:T(8,128)(2,1)}), bf16[2048,2048]{1,0:T(8,128)(2,1)}) %all-gather.28.cloned.1.call-update) | async-done | bytes 8388624 | tf_op jit(solution)/shard_map/all_gather | solution.py:160
  628.1 7.4 fusion.90
  638.7 25.4 %all-gather.32.cloned.1.call-done = bf16[2048,1024]{1,0:T(8,128)(2,1)} async-done(((bf16[512,1024]{1,0:T(8,128)(2,1)}), bf16[2048,1024]{1,0:T(8,128)(2,1)}) %all-gather.32.cloned.1.call-update) | async-done | bytes 4194320 | tf_op jit(solution)/shard_map/all_gather | solution.py:161
  664.1 127.7 %all-gather.30.cloned.1.call-done = bf16[1,2048,2048]{2,1,0:T(8,128)(2,1)} async-done(((bf16[1,256,2048]{2,1,0:T(8,128)(2,1)}), bf16[1,2048,2048]{2,1,0:T(8,128)(2,1)}) %all-gather.30.cloned.1.call-update) | async-done | bytes 8388624 | tf_op jit(solution)/shard_map/all_gather | solution.py:195
  791.8 14.5 fusion.19
  806.3 19.7 all-gather.34.cloned.1.call-done
  826.1 15.4 convert_bitcast_fusion.2
  841.6 111.4 %all-gather.36.cloned.1.call-done = bf16[1,2048,2048]{2,1,0:T(8,128)(2,1)} async-done(((bf16[1,256,2048]{2,1,0:T(8,128)(2,1)}), bf16[1,2048,2048]{2,1,0:T(8,128)(2,1)}) %all-gather.36.cloned.1.call-update) | async-done | bytes 8388624 | tf_op jit(solution)/shard_map/all_gather | solution.py:218
  953.0 21.0 convert_reduce_fusion
  974.0 2.0 copy-done.57
  976.0 10.9 convert_bitcast_fusion.1
  987.6 5.6 all-gather.6
  993.2 110.7 %reduce-scatter.11.cloned.1.call-done = bf16[1,256,2048]{2,1,0:T(8,128)(2,1)} async-done(((bf16[1,2048,2048]{2,1,0:T(8,128)(2,1)}), bf16[1,256,2048]{2,1,0:T(8,128)(2,1)}) %reduce-scatter.11.cloned.1.call-update) | async-done | bytes 1048592 | tf_op jit(solution)/shard_map/reduce_scatter | solution.py:203
  1103.8 151.9 %reduce-scatter.13.cloned.1.call-done = bf16[1,256,2048]{2,1,0:T(8,128)(2,1)} async-done(((bf16[1,2048,2048]{2,1,0:T(8,128)(2,1)}), bf16[1,256,2048]{2,1,0:T(8,128)(2,1)}) %reduce-scatter.13.cloned.1.call-update) | async-done | bytes 1048592 | tf_op jit(solution)/shard_map/reduce_scatter | solution.py:232
  1255.8 5.1 fusion.55
  1263.9 5.7 convolution_convert_fusion.2
  1270.2 24.5 %multiply_reduce_fusion = (f32[16,256]{1,0:T(8,128)S(1)}, f32[16,256,2048]{2,1,0:T(8,128)}) fusion(f32[16,256,2048]{2,1,0:T(8,128)} %get-tuple-element.109, f32[16,256]{1,0:T(8,128)S(1)} %get-tuple-element.108, bf16[256,16,128]{0,2,1:T(8,128)(2,1)S(1)} %bitcast.149, bf16[1,2048,16,128]{1,3,2,0:T(8,128)(2,1)} %all-gather.22.cloned.1.call-done), kind=kOutput, calls=%fused_computation.2 | convolution fusion | flops 2172645376 | bytes 76578816 | tf_op jit(solution)/shard_map/while/body/eval_jaxpr/chd,khd->hck/dot_general | solution.py:83
  1294.7 27.7 %multiply_convert_fusion = bf16[16,256,2048]{2,1,0:T(8,128)(2,1)} fusion(f32[16,256,2048]{2,1,0:T(8,128)} %get-tuple-element.112, f32[16,256]{1,0:T(8,128)S(1)} %get-tuple-element.111, f32[16,256,2048]{2,1,0:T(8,128)} %get-tuple-element.109, f32[16,256]{1,0:T(8,128)S(1)} %get-tuple-element.108), kind=kLoop, calls=%fused_computation.1 | loop fusion | flops 33554432 | bytes 83918848 | tf_op jit(solution)/shard_map/while/body/eval_jaxpr/convert_element_type | solution.py:89
  1322.3 12.1 fusion.12
  1335.6 16.2 convert_bitcast_fusion
  1353.1 5.6 convolution_convert_fusion.1
  1358.7 10.8 multiply_bitcast_fusion
  1369.6 113.4 %reduce-scatter.15.cloned.1.call-done = bf16[1,256,16,128]{3,1,2,0:T(8,128)(2,1)} async-done(((bf16[1,2048,16,128]{3,1,2,0:T(8,128)(2,1)}), bf16[1,256,16,128]{3,1,2,0:T(8,128)(2,1)}) %reduce-scatter.15.cloned.1.call-update) | async-done | bytes 1048592 | tf_op jit(solution)/shard_map/reduce_scatter | solution.py:252
  1484.4 3.1 multiply_add_fusion.3
  1488.8 4.2 add_convert_fusion
  1494.6 140.7 %reduce-scatter.17.cloned.1.call-done = bf16[1,256,16,128]{1,3,2,0:T(8,128)(2,1)} async-done(((bf16[1,2048,16,128]{1,3,2,0:T(8,128)(2,1)}), bf16[1,256,16,128]{1,3,2,0:T(8,128)(2,1)}) %reduce-scatter.17.cloned.1.call-update) | async-done | bytes 1048592 | tf_op jit(solution)/shard_map/reduce_scatter | solution.py:255
  1635.3 14.9 convolution_convert_fusion
  1650.9 16.8 fusion.35
  1667.8 14.3 fusion.38
  1682.1 26.4 %reduce-scatter.23.cloned.1.call-done = bf16[512,2048]{1,0:T(8,128)(2,1)} async-done(((bf16[2048,2048]{1,0:T(8,128)(2,1)}), bf16[512,2048]{1,0:T(8,128)(2,1)}) %reduce-scatter.23.cloned.1.call-update) | async-done | bytes 2097168 | tf_op jit(solution)/shard_map/reduce_scatter | solution.py:282
  1708.8 182.8 %reduce-scatter.19.cloned.1.call-done = bf16[512,6144]{1,0:T(8,128)(2,1)} async-done(((bf16[2048,6144]{1,0:T(8,128)(2,1)}), bf16[512,6144]{1,0:T(8,128)(2,1)}) %reduce-scatter.19.cloned.1.call-update) | async-done | bytes 6291472 | tf_op jit(solution)/shard_map/reduce_scatter | solution.py:279
  1891.6 1.6 copy-done.15
  1894.7 43.8 %reduce-scatter.29.cloned.1.call-done = bf16[1024,512]{1,0:T(8,128)(2,1)} async-done(((bf16[1024,2048]{1,0:T(8,128)(2,1)}), bf16[1024,512]{1,0:T(8,128)(2,1)}) %reduce-scatter.29.cloned.1.call-update) | async-done | bytes 1048592 | tf_op jit(solution)/shard_map/reduce_scatter | solution.py:288
  1938.5 2.8 convert_element_type.258
  1941.3 44.3 %reduce-scatter.27.cloned.1.call-done = bf16[512,1024]{1,0:T(8,128)(2,1)} async-done(((bf16[2048,1024]{1,0:T(8,128)(2,1)}), bf16[512,1024]{1,0:T(8,128)(2,1)}) %reduce-scatter.27.cloned.1.call-update) | async-done | bytes 1048592 | tf_op jit(solution)/shard_map/reduce_scatter | solution.py:285
  1985.6 2.8 convert_element_type.255
  1988.4 1.9 pad_maximum_fusion.7
  1990.3 14.4 fusion.54
  2007.8 2.4 convert_reduce_fusion.4
  2010.2 41.7 %all-reduce.6 = (f32[2048]{0:T(1024)}, f32[2048]{0:T(1024)}, f32[6144]{0:T(1024)}, f32[2048]{0:T(1024)}, f32[2048]{0:T(1024)}, /*index=5*/f32[2048]{0:T(1024)}, ...) all-reduce(f32[2048]{0:T(1024)S(1)} %get-tuple-element.60, ...), channel_id=1, replica_groups=mesh['dp'=4,'seq'=8] {'dp','seq'}, use_global_device_ids=true, to_apply=%region_18.19 | all-reduce | flops 26628 | bytes 213024 | tf_op jit(solution)/shard_map/psum | solution.py:311
  2053.0 3.7 reduce-scatter.25.cloned.1.call-done
  2056.8 1.8 convert_element_type.252
  2058.5 118.7 %reduce-scatter.21.cloned.1.call-done = bf16[64,6144]{1,0:T(8,128)(2,1)} async-done(((bf16[512,6144]{1,0:T(8,128)(2,1)}), bf16[64,6144]{1,0:T(8,128)(2,1)}) %reduce-scatter.21.cloned.1.call-update) | async-done | bytes 786448 | tf_op jit(solution)/shard_map/reduce_scatter | solution.py:293
  2177.2 2.4 convert_element_type.249
  (211 shorter events, 30.4 us)
Async XLA Ops:
  7.2 104.8 %all-gather.18.cloned.1.call-start = ((), (), s32[]{:S(2)}) async-start(), calls=%async_computation.10 | async-start | bytes 7077888 | tf_op jit(solution)/shard_map/all_gather | solution.py:143
  7.9 258.7 %all-gather.20.cloned.1.call-start = ((), (), s32[]{:S(2)}) async-start(), calls=%async_computation.11 | async-start | bytes 31457280 | tf_op jit(solution)/shard_map/all_gather | solution.py:159
  112.0 2.4 copy-start.51
  112.0 12.8 copy-start.45
  112.0 12.8 copy-start.33
  112.0 206.0 %all-gather.26.cloned.1.call-start = ((), (), s32[]{:S(2)}) async-start(), calls=%async_computation.14 | async-start | bytes 2359296 | tf_op jit(solution)/shard_map/all_gather | solution.py:144
  112.7 331.3 %all-gather.24.cloned.1.call-start = ((), (), s32[]{:S(2)}) async-start(), calls=%async_computation.13 | async-start | bytes 9437184 | tf_op jit(solution)/shard_map/all_gather | solution.py:185
  113.4 165.0 %copy-start.29 = (f32[256]{0:T(256)}, f32[256]{0:T(256)S(1)}, u32[]{:S(2)}) copy-start(f32[256]{0:T(256)S(1)} %broadcast_multiply_fusion.1) | copy-start | bytes 3076
  113.9 164.5 %copy-start.31 = (f32[256]{0:T(256)}, f32[256]{0:T(256)S(1)}, u32[]{:S(2)}) copy-start(f32[256]{0:T(256)S(1)} %fusion.77) | copy-start | bytes 3076
  119.5 158.9 %copy-start.27 = (f32[4,1,512]{2,1,0:T(1,128)}, f32[4,1,512]{2,1,0:T(1,128)S(1)}, u32[]{:S(2)}) copy-start(f32[4,1,512]{2,1,0:T(1,128)S(1)} %convert_element_type.261) | copy-start | bytes 24580
  124.7 153.7 %copy-start.25 = (f32[4,1,512]{2,1,0:T(1,128)}, f32[4,1,512]{2,1,0:T(1,128)S(1)}, u32[]{:S(2)}) copy-start(f32[4,1,512]{2,1,0:T(1,128)S(1)} %convert_element_type.260) | copy-start | bytes 24580
  131.4 151.9 %copy-start.19 = (f32[256,64]{1,0:T(8,128)}, f32[256,64]{1,0:T(8,128)S(1)}, u32[]{:S(2)}) copy-start(f32[256,64]{1,0:T(8,128)S(1)} %get-tuple-element.106) | copy-start | bytes 196612
  131.4 151.9 %copy-start.21 = (f32[256,64]{1,0:T(8,128)}, f32[256,64]{1,0:T(8,128)S(1)}, u32[]{:S(2)}) copy-start(f32[256,64]{1,0:T(8,128)S(1)} %get-tuple-element.107) | copy-start | bytes 196612
  278.4 2.8 copy-start.16
  286.1 158.0 %copy-start.4 = (bf16[256,16,64]{2,0,1:T(8,128)(2,1)}, bf16[256,16,64]{2,0,1:T(8,128)(2,1)S(1)}, u32[]{:S(2)}) copy-start(bf16[256,16,64]{2,0,1:T(8,128)(2,1)S(1)} %get-tuple-element.86) | copy-start | bytes 1572868
  286.1 158.0 %copy-start.6 = (bf16[256,16,64]{2,0,1:T(8,128)(2,1)}, bf16[256,16,64]{2,0,1:T(8,128)(2,1)S(1)}, u32[]{:S(2)}) copy-start(bf16[256,16,64]{2,0,1:T(8,128)(2,1)S(1)} %get-tuple-element.87) | copy-start | bytes 1572868
  287.8 282.4 %all-gather.22.cloned.1.call-start = ((), (), s32[]{:S(2)}) async-start(), calls=%async_computation.12 | async-start | bytes 9437184 | tf_op jit(solution)/shard_map/all_gather | solution.py:186
  290.5 28.9 %copy-start.52 = (bf16[512]{0:T(512)(128)(2,1)S(1)}, bf16[512]{0:T(512)(128)(2,1)}, u32[]{:S(2)}) copy-start(bf16[512]{0:T(512)(128)(2,1)} %param.22) | copy-start | bytes 3076
  290.5 28.9 %copy-start.53 = (bf16[512]{0:T(512)(128)(2,1)S(1)}, bf16[512]{0:T(512)(128)(2,1)}, u32[]{:S(2)}) copy-start(bf16[512]{0:T(512)(128)(2,1)} %param.23) | copy-start | bytes 3076
  290.5 28.9 %copy-start.54 = (bf16[512]{0:T(512)(128)(2,1)S(1)}, bf16[512]{0:T(512)(128)(2,1)}, u32[]{:S(2)}) copy-start(bf16[512]{0:T(512)(128)(2,1)} %param.24) | copy-start | bytes 3076
  292.9 335.2 %all-gather.28.cloned.1.call-start = ((), (), s32[]{:S(2)}) async-start(), calls=%async_computation.15 | async-start | bytes 10485760 | tf_op jit(solution)/shard_map/all_gather | solution.py:160
  318.0 346.1 %all-gather.32.cloned.1.call-start = ((), (), s32[]{:S(2)}) async-start(), calls=%async_computation.17 | async-start | bytes 5242880 | tf_op jit(solution)/shard_map/all_gather | solution.py:161
  318.8 473.0 %all-gather.30.cloned.1.call-start = ((), (), s32[]{:S(2)}) async-start(), calls=%async_computation.16 | async-start | bytes 9437184 | tf_op jit(solution)/shard_map/all_gather | solution.py:195
  319.5 124.6 %copy-start.41 = (s32[1,256]{1,0:T(1,128)}, s32[1,256]{1,0:T(1,128)S(1)}, u32[]{:S(2)}) copy-start(s32[1,256]{1,0:T(1,128)S(1)} %get-tuple-element.77) | copy-start | bytes 3076
  635.9 2.8 copy-start.47
  637.3 188.7 %all-gather.34.cloned.1.call-start = ((), (), s32[]{:S(2)}) async-start(), calls=%async_computation.18 | async-start | bytes 5242880 | tf_op jit(solution)/shard_map/all_gather | solution.py:162
  638.1 314.9 %all-gather.36.cloned.1.call-start = ((), (), s32[]{:S(2)}) async-start(), calls=%async_computation.20 | async-start | bytes 9437184 | tf_op jit(solution)/shard_map/all_gather | solution.py:218
  638.6 465.2 %reduce-scatter.11.cloned.1.call-start = ((), (), s32[]{:S(2)}) async-start(), calls=%async_computation.19 | async-start | bytes 9437184 | tf_op jit(solution)/shard_map/reduce_scatter | solution.py:203
  638.7 314.3 %copy-start.43 = (f32[1024]{0:T(1024)}, f32[1024]{0:T(1024)S(1)}, u32[]{:S(2)}) copy-start(f32[1024]{0:T(1024)S(1)} %convert_element_type.226) | copy-start | bytes 12292
  841.5 414.3 %reduce-scatter.13.cloned.1.call-start = ((), (), s32[]{:S(2)}) async-start(), calls=%async_computation.21 | async-start | bytes 9437184 | tf_op jit(solution)/shard_map/reduce_scatter | solution.py:232
  953.0 23.0 %copy-start.56 = (bf16[2048,1024]{1,0:T(8,128)(2,1)S(1)}, bf16[2048,1024]{1,0:T(8,128)(2,1)}, u32[]{:S(2)}) copy-start(bf16[2048,1024]{1,0:T(8,128)(2,1)} %all-gather.32.cloned.1.call-done) | copy-start | bytes 12582916
  986.9 6.2 copy-start.42
  986.9 496.1 %reduce-scatter.15.cloned.1.call-start = ((), (), s32[]{:S(2)}) async-start(), calls=%async_computation.22 | async-start | bytes 9437184 | tf_op jit(solution)/shard_map/reduce_scatter | solution.py:252
  993.2 267.7 %copy-start.48 = (pred[256]{0:T(512)(128)(4,1)}, pred[256]{0:T(512)(128)(4,1)S(1)}, u32[]{:S(2)}) copy-start(pred[256]{0:T(512)(128)(4,1)S(1)} %compare_reduce_fusion) | copy-start | bytes 772
  1255.8 5.1 copy-start.18
  1260.8 2.1 copy-start.12
  1261.6 8.1 copy-start.37
  1270.2 24.5 %copy-start.23 = (bf16[256,2048]{0,1:T(8,128)(2,1)}, bf16[256,2048]{0,1:T(8,128)(2,1)S(1)}, u32[]{:S(2)}) copy-start(bf16[256,2048]{0,1:T(8,128)(2,1)S(1)} %copy.84) | copy-start | bytes 3145732
  1294.7 27.7 %copy-start.5 = (bf16[256,16,64]{2,0,1:T(8,128)(2,1)S(1)}, bf16[256,16,64]{2,0,1:T(8,128)(2,1)}, u32[]{:S(2)}) copy-start(bf16[256,16,64]{2,0,1:T(8,128)(2,1)} %copy-done.4) | copy-start | bytes 1572868
  1294.7 27.7 %copy-start.7 = (bf16[256,16,64]{2,0,1:T(8,128)(2,1)S(1)}, bf16[256,16,64]{2,0,1:T(8,128)(2,1)}, u32[]{:S(2)}) copy-start(bf16[256,16,64]{2,0,1:T(8,128)(2,1)} %copy-done.6) | copy-start | bytes 1572868
  1334.4 300.9 %reduce-scatter.17.cloned.1.call-start = ((), (), s32[]{:S(2)}) async-start(), calls=%async_computation.23 | async-start | bytes 9437184 | tf_op jit(solution)/shard_map/reduce_scatter | solution.py:255
  1351.9 356.6 %reduce-scatter.23.cloned.1.call-start = ((), (), s32[]{:S(2)}) async-start(), calls=%async_computation.26 | async-start | bytes 10485760 | tf_op jit(solution)/shard_map/reduce_scatter | solution.py:282
  1358.7 532.9 %reduce-scatter.19.cloned.1.call-start = ((), (), s32[]{:S(2)}) async-start(), calls=%async_computation.24 | async-start | bytes 31457280 | tf_op jit(solution)/shard_map/reduce_scatter | solution.py:279
  1369.5 114.9 %copy-start.20 = (f32[256,64]{1,0:T(8,128)S(1)}, f32[256,64]{1,0:T(8,128)}, u32[]{:S(2)}) copy-start(f32[256,64]{1,0:T(8,128)} %copy-done.19) | copy-start | bytes 196612
  1369.5 114.9 %copy-start.22 = (f32[256,64]{1,0:T(8,128)S(1)}, f32[256,64]{1,0:T(8,128)}, u32[]{:S(2)}) copy-start(f32[256,64]{1,0:T(8,128)} %copy-done.21) | copy-start | bytes 196612
  1488.7 146.6 %copy-start.8 = (bf16[1,256,16,128]{1,3,2,0:T(8,128)(2,1)}, bf16[1,256,16,128]{1,3,2,0:T(8,128)(2,1)S(1)}, u32[]{:S(2)}) copy-start(bf16[1,256,16,128]{1,3,2,0:T(8,128)(2,1)S(1)} %copy.67) | copy-start | bytes 3145732
  1488.7 146.6 %copy-start.1 = (bf16[1,256,2048]{2,1,0:T(8,128)(2,1)S(1)}, bf16[1,256,2048]{2,1,0:T(8,128)(2,1)}, u32[]{:S(2)}) copy-start(bf16[1,256,2048]{2,1,0:T(8,128)(2,1)} %param.15) | copy-start | bytes 3145732
  1488.7 146.6 %copy-start.26 = (f32[4,1,512]{2,1,0:T(1,128)S(1)}, f32[4,1,512]{2,1,0:T(1,128)}, u32[]{:S(2)}) copy-start(f32[4,1,512]{2,1,0:T(1,128)} %copy-done.25) | copy-start | bytes 24580
  1488.8 146.5 %copy-start.28 = (f32[4,1,512]{2,1,0:T(1,128)S(1)}, f32[4,1,512]{2,1,0:T(1,128)}, u32[]{:S(2)}) copy-start(f32[4,1,512]{2,1,0:T(1,128)} %copy-done.27) | copy-start | bytes 24580
  1488.8 146.5 %copy-start.30 = (f32[256]{0:T(256)S(1)}, f32[256]{0:T(256)}, u32[]{:S(2)}) copy-start(f32[256]{0:T(256)} %copy-done.29) | copy-start | bytes 3076
  1488.8 146.5 %copy-start.32 = (f32[256]{0:T(256)S(1)}, f32[256]{0:T(256)}, u32[]{:S(2)}) copy-start(f32[256]{0:T(256)} %copy-done.31) | copy-start | bytes 3076
  1494.5 155.7 %copy-start.10 = (bf16[1,256,16,128]{1,3,2,0:T(8,128)(2,1)}, bf16[1,256,16,128]{1,3,2,0:T(8,128)(2,1)S(1)}, u32[]{:S(2)}) copy-start(bf16[1,256,16,128]{1,3,2,0:T(8,128)(2,1)S(1)} %copy.70) | copy-start | bytes 3145732
  1650.2 288.3 %reduce-scatter.29.cloned.1.call-start = ((), (), s32[]{:S(2)}) async-start(), calls=%async_computation.29 | async-start | bytes 5242880 | tf_op jit(solution)/shard_map/reduce_scatter | solution.py:288
  1667.7 317.9 %reduce-scatter.27.cloned.1.call-start = ((), (), s32[]{:S(2)}) async-start(), calls=%async_computation.28 | async-start | bytes 5242880 | tf_op jit(solution)/shard_map/reduce_scatter | solution.py:285
  1682.1 374.7 %reduce-scatter.25.cloned.1.call-start = ((), (), s32[]{:S(2)}) async-start(), calls=%async_computation.27 | async-start | bytes 2359296 | tf_op jit(solution)/shard_map/reduce_scatter | solution.py:296
  1708.5 468.7 %reduce-scatter.21.cloned.1.call-start = ((), (), s32[]{:S(2)}) async-start(), calls=%async_computation.25 | async-start | bytes 7077888 | tf_op jit(solution)/shard_map/reduce_scatter | solution.py:293
  1891.6 2.8 copy-start.46
  1990.3 14.6 copy-start.40
  2004.9 2.8 copy-start.3
  2004.9 2.8 copy-start.13
  2004.9 2.8 copy-start.38
  2007.7 2.4 copy-start.34
  2007.7 2.4 copy-start.35
  2007.8 2.4 copy-start.36
  (14 other events, 18.7 us)
Sparse Core Ops, SparseCore 0:
  10.2 101.7 all-gather.17
  113.5 153.0 all-gather.19
  268.8 49.2 all-gather.25
  320.6 123.3 all-gather.23
  446.5 123.5 all-gather.21
  571.6 56.4 all-gather.27
  629.6 34.4 all-gather.31
  666.8 124.9 all-gather.29
  793.4 32.6 all-gather.33
  828.0 124.9 all-gather.35
  956.6 147.1 reduce-scatter.10
  1107.8 147.9 reduce-scatter.12
  1334.5 148.4 reduce-scatter.14
  1486.9 148.3 reduce-scatter.16
  1637.7 70.7 reduce-scatter.22
  1711.1 180.4 reduce-scatter.18
  1894.0 44.4 reduce-scatter.28
  1941.0 44.5 reduce-scatter.26
  1989.1 67.5 reduce-scatter.24
  2060.2 116.9 reduce-scatter.20
where the time goes:
time: 2200 us; the launch traced here: 2190 us
  waiting for transfers between devices  1700 us (77%)
  matrix products  253 us (12%)
  other arithmetic  110 us (5%)
  blocking collectives  78.7 us (4%)
  local copies, waits for them, and re-layouts  22.8 us (1%)
    reduce_scatter x1, waiting for transfers between devices, local(): lax.psum_scatter(qkv_weight_grad.astype(jnp.bfloat16), 'dp', scatter_dime...  183 us
    reduce_scatter x1, waiting for transfers between devices, local(): lax.psum_scatter(normed_terms.astype(jnp.bfloat16), 'seq', scatter_dimens...  152 us
    reduce_scatter x1, waiting for transfers between devices, local(): lax.psum_scatter(value_grad_all.astype(jnp.bfloat16), 'seq', scatter_dime...  141 us
    all_gather x1, waiting for transfers between devices, local(): lax.all_gather(qkv_rows, 'dp', axis=0, tiled=True)  135 us
    all_gather x1, waiting for transfers between devices, local(): normed_full = lax.all_gather(normed_two, 'seq', axis=1, tiled=True)  128 us
    reduce_scatter x1, waiting for transfers between devices, local(): lax.psum_scatter(qkv_grad_rows.astype(jnp.bfloat16), 'seq', scatter_dimen...  119 us
    reduce_scatter x1, waiting for transfers between devices, local(): lax.psum_scatter(key_grad_all.astype(jnp.bfloat16), 'seq', scatter_dimens...  113 us
    all_gather x1, waiting for transfers between devices, local(): low_full = lax.all_gather(cotangent, 'seq', axis=1, tiled=True)  111 us
  transfers between devices with their start and end apart: 20, of which 20 were waited for; matrix products, arithmetic and copies ran while one was open for 13% of the time, Pallas kernels for 0%

commit v1 on v0

--- a/solution.py
+++ b/solution.py
@@ -1,6 +1,11 @@
+import functools
+
 import jax
 import jax.numpy as jnp
 from jax import lax
+from jax.experimental import pallas as pl
+from jax.experimental.pallas import tpu as pltpu
+from jax.sharding import Mesh
 from jax.sharding import PartitionSpec as P
 
 HEADS = 16
@@ -343,7 +348,574 @@
     )
 
 
+PLANE_OF = (0, 3, 1, 2)
+ROW_OF = (0, 2, 3, 1)
+AXES = ("y", "core", "z", "x")
+PLANE = ("y", "core", "x")
+SWAP = [(0, 1), (1, 0)]
+LOG2E = 1.4426950408889634
+
+
+def trade(value, axis):
+    return lax.ppermute(value, axis, SWAP)
+
+
+def to_plane(value):
+    pairs = []
+    for r in range(4):
+        for z in range(4):
+            for x in range(2):
+                pairs.append(((r * 4 + z) * 2 + x, (ROW_OF[z] * 4 + PLANE_OF[r]) * 2 + x))
+    return lax.ppermute(value, AXES, pairs)
+
+
+def gather_plane(block):
+    half = block.shape[0] // 2
+    from_x = trade(block, "x")
+    from_y = trade(block, "y")
+    top = trade(from_y[:half], "x")
+    bottom = trade(from_x[half:], "y")
+    return jnp.concatenate(
+        [
+            block,
+            trade(block, "core"),
+            from_y,
+            trade(from_y, "core"),
+            from_x,
+            trade(from_x, "core"),
+            top,
+            bottom,
+            trade(top, "core"),
+            trade(bottom, "core"),
+        ],
+        axis=0,
+    )
+
+
+def scatter_plane(terms):
+    f32 = jnp.float32
+    span = terms.shape[0] // 8
+    half = span // 2
+    both = terms.reshape(2, 2, 2, span, -1)
+    mate = trade(both[:, :, 1], "core")
+    mine = (both[:, :, 0].astype(f32) + mate.astype(f32)).astype(jnp.bfloat16)
+    across_x = trade(mine[1, 1, :half], "x")
+    across_y = trade(mine[1, 1, half:], "y")
+    x_top = trade(mine[1, 0, :half], "x")
+    y_bottom = trade(mine[0, 1, half:], "y")
+    y_top = trade((mine[0, 1, :half].astype(f32) + across_x.astype(f32)).astype(jnp.bfloat16), "y")
+    x_bottom = trade((mine[1, 0, half:].astype(f32) + across_y.astype(f32)).astype(jnp.bfloat16), "x")
+    own = mine[0, 0].astype(f32)
+    return own + jnp.concatenate(
+        [x_top.astype(f32) + y_top.astype(f32), x_bottom.astype(f32) + y_bottom.astype(f32)], axis=0
+    )
+
+
+def norm_parts(values):
+    average = jnp.mean(values, axis=-1, keepdims=True)
+    centered = values - average
+    scale = lax.rsqrt(jnp.mean(centered * centered, axis=-1, keepdims=True) + EPSILON)
+    return centered * scale, scale
+
+
+def norm_back(unit, scale, gain_vec, grad):
+    unit_grad = grad * gain_vec
+    inner = unit_grad - jnp.mean(unit_grad, axis=-1, keepdims=True)
+    inner = inner - unit * jnp.mean(unit_grad * unit, axis=-1, keepdims=True)
+    return scale * inner, jnp.sum(grad * unit, axis=0), jnp.sum(grad, axis=0)
+
+
+def turn(values, cosine, sine, sign):
+    return values * cosine + sign * pltpu.roll(values, 64, 1) * sine
+
+
+CONTRACT_LAST = (((1,), (1,)), ((), ()))
+CONTRACT_FIRST = (((0,), (0,)), ((), ()))
+
+
+def attend_kernel(slot_of, first_of, qkv_ref, begin_ref, out_ref, lse_ref, turned, *, tile, scale):
+    i = pl.program_id(0)
+    f32 = jnp.float32
+
+    @pl.when(i == 0)
+    def _():
+        for h in range(2):
+            whole = qkv_ref[:, 512 + 128 * h : 640 + 128 * h]
+            turned[h] = whole.astype(f32).T.astype(jnp.bfloat16)
+
+    begin = begin_ref[0]
+    row = lax.broadcasted_iota(jnp.int32, (tile, tile), 0)
+    col = lax.broadcasted_iota(jnp.int32, (tile, tile), 1)
+    at = pl.multiple_of(slot_of[i] * tile, tile)
+    queries = [qkv_ref[pl.ds(at, tile), 128 * h : 128 * h + 128] for h in range(2)]
+
+    def scores(h, j, allowed):
+        there = pl.multiple_of(slot_of[j] * tile, tile)
+        keys = qkv_ref[pl.ds(there, tile), 256 + 128 * h : 384 + 128 * h]
+        found = lax.dot_general(keys, queries[h], CONTRACT_LAST, preferred_element_type=f32) * scale
+        return jnp.where(allowed, found, NEG_FILL), turned[h, :, pl.ds(there, tile)]
+
+    state = []
+    for h in range(2):
+        found, values = scores(h, i, (row <= col) & (row + i * tile >= begin))
+        top = jnp.max(found, axis=0, keepdims=True)
+        weights = jnp.exp2(found - top)
+        state.append(
+            (
+                top,
+                jnp.sum(weights, axis=0, keepdims=True),
+                jnp.dot(values, weights.astype(jnp.bfloat16), preferred_element_type=f32),
+            )
+        )
+
+    def step(j, state):
+        after = []
+        allowed = row + j * tile >= begin
+        for h in range(2):
+            top, total, sums = state[h]
+            found, values = scores(h, j, allowed)
+            higher = jnp.maximum(top, jnp.max(found, axis=0, keepdims=True))
+            shrink = jnp.exp2(top - higher)
+            weights = jnp.exp2(found - higher)
+            after.append(
+                (
+                    higher,
+                    total * shrink + jnp.sum(weights, axis=0, keepdims=True),
+                    sums * shrink
+                    + jnp.dot(values, weights.astype(jnp.bfloat16), preferred_element_type=f32),
+                )
+            )
+        return tuple(after)
+
+    state = lax.fori_loop(first_of[i], i, step, tuple(state))
+    for h in range(2):
+        top, total, sums = state[h]
+        out_ref[:, 128 * h : 128 * h + 128] = (sums / total).T.astype(jnp.bfloat16)
+        lse_ref[0, h : h + 1, :] = top + jnp.log2(total)
+
+
+def attend_back_kernel(
+    slot_of,
+    first_of,
+    qkv_ref,
+    begin_ref,
+    lse_ref,
+    out_ref,
+    grad_ref,
+    cos_ref,
+    sin_ref,
+    back_ref,
+    key_sums,
+    value_sums,
+    *,
+    tile,
+    scale,
+    plain,
+):
+    i = pl.program_id(0)
+    f32 = jnp.float32
+
+    @pl.when(i == 0)
+    def _():
+        key_sums[...] = jnp.zeros_like(key_sums)
+        value_sums[...] = jnp.zeros_like(value_sums)
+
+    begin = begin_ref[0]
+    row = lax.broadcasted_iota(jnp.int32, (tile, tile), 0)
+    col = lax.broadcasted_iota(jnp.int32, (tile, tile), 1)
+    at = pl.multiple_of(slot_of[i] * tile, tile)
+    queries = [qkv_ref[pl.ds(at, tile), 128 * h : 128 * h + 128] for h in range(2)]
+    grads = [grad_ref[:, 128 * h : 128 * h + 128] for h in range(2)]
+    inner = []
+    for h in range(2):
+        both = grads[h].astype(f32) * out_ref[:, 128 * h : 128 * h + 128].astype(f32)
+        inner.append(jnp.sum(both.T, axis=0, keepdims=True))
+
+    def pair(h, j, allowed, sums):
+        there = pl.multiple_of(slot_of[j] * tile, tile)
+        keys = qkv_ref[pl.ds(there, tile), 256 + 128 * h : 384 + 128 * h]
+        values = qkv_ref[pl.ds(there, tile), 512 + 128 * h : 640 + 128 * h]
+        found = lax.dot_general(keys, queries[h], CONTRACT_LAST, preferred_element_type=f32) * scale
+        weights = jnp.where(allowed, jnp.exp2(found - lse_ref[0, h : h + 1, :]), 0.0)
+        weight_grad = lax.dot_general(values, grads[h], CONTRACT_LAST, preferred_element_type=f32)
+        score_low = (weights * (weight_grad - inner[h])).astype(jnp.bfloat16)
+        value_sums[h, pl.ds(there, tile), :] += jnp.dot(
+            weights.astype(jnp.bfloat16), grads[h], preferred_element_type=f32
+        )
+        key_sums[h, pl.ds(there, tile), :] += jnp.dot(
+            score_low, queries[h], preferred_element_type=f32
+        )
+        return sums + lax.dot_general(score_low, keys, CONTRACT_FIRST, preferred_element_type=f32)
+
+    state = []
+    for h in range(2):
+        state.append(
+            pair(h, i, (row <= col) & (row + i * tile >= begin), jnp.zeros((tile, 128), f32))
+        )
+
+    def step(j, state):
+        allowed = row + j * tile >= begin
+        return tuple(pair(h, j, allowed, state[h]) for h in range(2))
+
+    state = lax.fori_loop(first_of[i], i, step, tuple(state))
+    cosine, sine = cos_ref[pl.ds(at, tile), :], sin_ref[pl.ds(at, tile), :]
+    for h in range(2):
+        back_ref[pl.ds(at, tile), 128 * h : 128 * h + 128] = (
+            turn(state[h] * plain, cosine, sine, -1.0)
+        ).astype(jnp.bfloat16)
+
+    @pl.when(i == pl.num_programs(0) - 1)
+    def _():
+        for h in range(2):
+            for s in range(8):
+                rows = pl.ds(s * tile, tile)
+                back_ref[rows, 256 + 128 * h : 384 + 128 * h] = turn(
+                    key_sums[h, rows, :] * plain, cos_ref[rows, :], sin_ref[rows, :], -1.0
+                ).astype(jnp.bfloat16)
+                back_ref[rows, 512 + 128 * h : 640 + 128 * h] = value_sums[h, rows, :].astype(
+                    jnp.bfloat16
+                )
+
+
+def attend(slot_of, first_of, qkv, begin):
+    length = qkv.shape[0]
+    tile = length // 8
+    return pl.pallas_call(
+        functools.partial(attend_kernel, tile=tile, scale=128**-0.5 * LOG2E),
+        out_shape=(
+            jax.ShapeDtypeStruct((length, 256), jnp.bfloat16),
+            jax.ShapeDtypeStruct((8, 2, tile), jnp.float32),
+        ),
+        grid_spec=pltpu.PrefetchScalarGridSpec(
+            num_scalar_prefetch=2,
+            grid=(8,),
+            in_specs=[
+                pl.BlockSpec((length, 768), lambda i, s, f: (0, 0)),
+                pl.BlockSpec((1, 1, tile), lambda i, s, f: (i, 0, 0)),
+            ],
+            out_specs=[
+                pl.BlockSpec((tile, 256), lambda i, s, f: (s[i], 0)),
+                pl.BlockSpec((1, 2, tile), lambda i, s, f: (i, 0, 0)),
+            ],
+            scratch_shapes=[pltpu.VMEM((2, 128, length), jnp.bfloat16)],
+        ),
+        compiler_params=pltpu.CompilerParams(vmem_limit_bytes=40 << 20),
+        cost_estimate=pl.CostEstimate(flops=3 << 30, bytes_accessed=5 << 20, transcendentals=5 << 20),
+        name="attend",
+    )(slot_of, first_of, qkv, begin)
+
+
+def attend_backward(slot_of, first_of, qkv, begin, lse, out, grad, cosine, sine):
+    length = qkv.shape[0]
+    tile = length // 8
+    return pl.pallas_call(
+        functools.partial(
+            attend_back_kernel, tile=tile, scale=128**-0.5 * LOG2E, plain=128**-0.5
+        ),
+        out_shape=jax.ShapeDtypeStruct((length, 768), jnp.bfloat16),
+        grid_spec=pltpu.PrefetchScalarGridSpec(
+            num_scalar_prefetch=2,
+            grid=(8,),
+            in_specs=[
+                pl.BlockSpec((length, 768), lambda i, s, f: (0, 0)),
+                pl.BlockSpec((1, 1, tile), lambda i, s, f: (i, 0, 0)),
+                pl.BlockSpec((1, 2, tile), lambda i, s, f: (i, 0, 0)),
+                pl.BlockSpec((tile, 256), lambda i, s, f: (s[i], 0)),
+                pl.BlockSpec((tile, 256), lambda i, s, f: (s[i], 0)),
+                pl.BlockSpec((length, 128), lambda i, s, f: (0, 0)),
+                pl.BlockSpec((length, 128), lambda i, s, f: (0, 0)),
+            ],
+            out_specs=pl.BlockSpec((length, 768), lambda i, s, f: (0, 0)),
+            scratch_shapes=[
+                pltpu.VMEM((2, length, 128), jnp.float32),
+                pltpu.VMEM((2, length, 128), jnp.float32),
+            ],
+        ),
+        compiler_params=pltpu.CompilerParams(vmem_limit_bytes=48 << 20),
+        cost_estimate=pl.CostEstimate(flops=8 << 30, bytes_accessed=12 << 20, transcendentals=5 << 20),
+        name="attend_back",
+    )(slot_of, first_of, qkv, begin, lse, out, grad, cosine, sine)
+
+
+def rotate_wide(values, cosine, sine):
+    length = values.shape[0]
+    heads = values.reshape(length, -1, 2, 64)
+    swapped = heads[:, :, ::-1]
+    turned = heads * cosine.reshape(length, 1, 2, 64) + swapped * sine.reshape(length, 1, 2, 64)
+    return turned.reshape(length, -1)
+
+
+def matmul(left, right, how="ab,bc->ac"):
+    return jnp.einsum(how, left, right, preferred_element_type=jnp.float32)
+
+
+def plane_local(
+    tokens,
+    segment_ids,
+    ln1_gain,
+    ln1_bias,
+    w_qkv,
+    b_qkv,
+    w_out,
+    b_out,
+    ln2_gain,
+    ln2_bias,
+    w_up,
+    b_up,
+    w_down,
+    b_down,
+    cotangent,
+):
+    f32, bf16 = jnp.float32, jnp.bfloat16
+    span, width = tokens.shape[1:]
+    length = segment_ids.shape[1]
+    my_y, my_core, my_z, my_x = (lax.axis_index(a) for a in AXES)
+    my_r = my_y * 2 + my_core
+    mine = my_r * 2 + my_x
+
+    stream_low = to_plane(tokens[0])
+    segments = to_plane(segment_ids)
+    cot_low = to_plane(cotangent[0])
+
+    piece = w_qkv.shape[0]
+    part = w_qkv.reshape(piece, 3, 8, 256).transpose(2, 0, 1, 3).reshape(8 * piece, 768)
+    part = lax.all_to_all(part, PLANE, 0, 0, tiled=True)
+    qkv_all = lax.all_gather(part, "z", axis=0, tiled=True)
+    qkv_weight = (
+        qkv_all.reshape(4, 4, 2, piece, 768).transpose(1, 0, 2, 3, 4).reshape(width, 768)
+    )
+    out_all = lax.all_gather(w_out, "z", axis=0, tiled=False)
+    low_half, high_half = out_all[:2], out_all[2:]
+    keep = jnp.where(my_x == 0, low_half, high_half)
+    give = jnp.where(my_x == 0, high_half, low_half)
+    got = trade(give, "x")
+    out_weight = jnp.stack(
+        [jnp.where(my_x == 0, keep, got), jnp.where(my_x == 0, got, keep)], axis=1
+    ).reshape(256, width)
+    quarter = w_up.shape[1] // 4
+    up_part = w_up.reshape(-1, 4, quarter).transpose(1, 0, 2)
+    up_part = lax.all_to_all(up_part, ("y", "core"), 0, 0, tiled=True).reshape(width, quarter)
+    up_weight = lax.all_gather(up_part, "z", axis=1, tiled=True)
+    down_part = lax.all_to_all(
+        w_down.reshape(4, quarter, -1), ("y", "core"), 0, 0, tiled=True
+    )
+    down_part = down_part.transpose(1, 0, 2).reshape(quarter, width)
+    down_weight = lax.all_gather(down_part, "z", axis=0, tiled=True)
+
+    small = jnp.concatenate([ln1_gain, ln1_bias, b_out, ln2_gain, ln2_bias, b_down, b_qkv, b_up])
+    small = lax.all_gather(small, ("y", "core", "z"), axis=0, tiled=False)
+    over_dp = small.reshape(4, 4, -1)[:, 0].astype(f32)
+    step = ln1_gain.shape[0]
+    gain_one, shift_one, out_bias, gain_two, shift_two, down_bias = (
+        over_dp[:, k * step : (k + 1) * step].reshape(width) for k in range(6)
+    )
+    qkv_bias_all = over_dp[:, 6 * step : 9 * step].reshape(3, 8, 256)
+    qkv_bias = lax.dynamic_index_in_dim(qkv_bias_all, mine, 1, keepdims=False).reshape(768)
+    up_bias = lax.dynamic_slice_in_dim(
+        small.reshape(4, 4, -1)[0, :, 9 * step :], my_r * quarter, quarter, 1
+    )
+    up_bias = up_bias.reshape(-1).astype(f32)
+
+    plane_of = jnp.array(PLANE_OF, jnp.int32)
+    slots = jnp.arange(8, dtype=jnp.int32)
+    rows_of_slots = (my_y ^ ((slots >> 1) & 1)) * 2 + (my_core ^ (slots & 1))
+    place_of = plane_of[rows_of_slots] * 2 + (my_x ^ (slots >> 2))
+    slot_of = jnp.sum(
+        jnp.where(place_of[None, :] == slots[:, None], slots[None, :], 0), axis=1
+    ).astype(jnp.int32)
+    places = positions_of(segments)[0]
+    begin = (jnp.arange(length, dtype=jnp.int32) - places).reshape(8, 1, span)
+    first_of = begin[:, 0, 0] // span
+    by_slot = jnp.take(places.reshape(8, span), place_of, axis=0).reshape(length)
+    freqs = 10000.0 ** (-jnp.arange(64, dtype=f32) / 64)
+    angles = by_slot.astype(f32)[:, None] * freqs
+    cos_half, sin_half = jnp.cos(angles), jnp.sin(angles)
+    cosine = jnp.concatenate([cos_half, cos_half], axis=1)
+    sine = jnp.concatenate([-sin_half, sin_half], axis=1)
+
+    stream = stream_low.astype(f32)
+    unit_one, scale_one = norm_parts(stream)
+    normed_one = (unit_one * gain_one + shift_one).astype(bf16)
+    normed_one_row = gather_plane(normed_one)
+    projected = matmul(normed_one_row, qkv_weight) + qkv_bias
+    qkv = jnp.concatenate(
+        [rotate_wide(projected[:, :512], cosine, sine), projected[:, 512:]], axis=1
+    ).astype(bf16)
+    attended, lse = attend(slot_of, first_of, qkv, begin)
+    attn_branch = scatter_plane(matmul(attended, out_weight).astype(bf16)) + out_bias
+    middle = stream + attn_branch
+
+    unit_two, scale_two = norm_parts(middle)
+    normed_two = (unit_two * gain_two + shift_two).astype(bf16)
+    normed_two_row = gather_plane(normed_two)
+    hidden_pre = matmul(normed_two_row, up_weight) + up_bias
+    activated = jax.nn.gelu(hidden_pre, approximate=True).astype(bf16)
+    mlp_branch = scatter_plane(matmul(activated, down_weight).astype(bf16)) + down_bias
+    output = middle + mlp_branch
+    my_places = plane_of[my_r] * 2 + my_x
+    valid = lax.dynamic_index_in_dim(segments.reshape(8, span), my_places, 0, keepdims=False) != 0
+    valid_rows = valid[:, None]
+    square_sums = jnp.stack(
+        [
+            jnp.sum(jnp.where(valid_rows, output * output, 0.0)),
+            jnp.sum(jnp.where(valid_rows, attn_branch * attn_branch, 0.0)),
+            jnp.sum(jnp.where(valid_rows, mlp_branch * mlp_branch, 0.0)),
+            jnp.sum(valid.astype(f32)),
+        ]
+    )
+    layer_output = to_plane(output.astype(bf16))
+
+    cot_row = gather_plane(cot_low)
+    out_grad = cot_low.astype(f32)
+    down_bias_grad = jnp.sum(out_grad, axis=0)
+    down_grad = matmul(activated, cot_row, "tf,td->fd")
+    act_grad = matmul(cot_row, down_weight, "td,fd->tf")
+    up_low = gelu_back(hidden_pre, act_grad).astype(bf16)
+    up_grad = matmul(normed_two_row, up_low, "td,tf->df")
+    up_bias_grad = jnp.sum(up_low.astype(f32), axis=0)
+    normed_two_grad = scatter_plane(matmul(up_low, up_weight, "tf,df->td").astype(bf16))
+    middle_part, gain_two_grad, shift_two_grad = norm_back(
+        unit_two, scale_two, gain_two, normed_two_grad
+    )
+    middle_grad = out_grad + middle_part
+
+    attn_low = middle_grad.astype(bf16)
+    attn_low_row = gather_plane(attn_low)
+    out_bias_grad = jnp.sum(attn_low.astype(f32), axis=0)
+    attended_grad = matmul(attn_low_row, out_weight, "td,ed->te").astype(bf16)
+    out_grad_part = matmul(attended, attn_low_row, "te,td->ed")
+    projected_low = attend_backward(
+        slot_of, first_of, qkv, begin, lse, attended, attended_grad, cosine, sine
+    )
+    qkv_grad = matmul(normed_one_row, projected_low, "td,te->de")
+    qkv_bias_grad = jnp.sum(projected_low.astype(f32), axis=0)
+    normed_one_grad = scatter_plane(matmul(projected_low, qkv_weight, "te,de->td").astype(bf16))
+    stream_part, gain_one_grad, shift_one_grad = norm_back(
+        unit_one, scale_one, gain_one, normed_one_grad
+    )
+    input_grad = to_plane((middle_grad + stream_part).astype(bf16)).astype(f32)
+
+    def over_z(value):
+        return lax.psum_scatter(value.astype(bf16), "z", scatter_dimension=0, tiled=True)
+
+    down_out = over_z(down_grad).reshape(quarter, 4, -1).transpose(1, 0, 2)
+    down_out = lax.all_to_all(down_out, ("y", "core"), 0, 0, tiled=True)
+    down_out = down_out.reshape(4 * quarter, -1).astype(f32)
+    up_out = over_z(up_grad.reshape(width, 4, quarter).transpose(1, 0, 2).reshape(-1, quarter))
+    up_out = lax.all_to_all(up_out.reshape(4, -1, quarter), ("y", "core"), 0, 0, tiled=True)
+    up_out = up_out.transpose(1, 0, 2).reshape(-1, 4 * quarter).astype(f32)
+    out_parts = out_grad_part.astype(bf16).reshape(2, 2, -1, width)
+    keep = jnp.where(my_x == 0, out_parts[:, 0], out_parts[:, 1])
+    give = jnp.where(my_x == 0, out_parts[:, 1], out_parts[:, 0])
+    got = trade(give, "x")
+    out_parts = jnp.concatenate(
+        [jnp.where(my_x == 0, keep, got), jnp.where(my_x == 0, got, keep)], axis=0
+    )
+    out_out = over_z(out_parts.reshape(-1, width)).astype(f32)
+    qkv_parts = qkv_grad.astype(bf16).reshape(4, 4, 2, piece, 768).transpose(1, 0, 2, 3, 4)
+    qkv_out = over_z(qkv_parts.reshape(width, 768))
+    qkv_out = lax.all_to_all(qkv_out, PLANE, 0, 0, tiled=True)
+    qkv_out = qkv_out.reshape(8, piece, 3, 256).transpose(1, 2, 0, 3).reshape(piece, -1).astype(f32)
+
+    qkv_bias_terms = lax.dynamic_update_slice(
+        jnp.zeros((3, 8, 256), f32), qkv_bias_grad.reshape(3, 1, 256), (0, mine, 0)
+    )
+    up_bias_terms = lax.dynamic_update_slice(
+        jnp.zeros((4, 2, 4, quarter), f32),
+        up_bias_grad.reshape(4, 1, 1, quarter),
+        (0, my_x, my_r, 0),
+    )
+    (
+        totals,
+        gain_one_total,
+        shift_one_total,
+        qkv_bias_total,
+        out_bias_total,
+        gain_two_total,
+        shift_two_total,
+        up_bias_total,
+        down_bias_total,
+    ) = lax.psum(
+        (
+            square_sums,
+            gain_one_grad,
+            shift_one_grad,
+            qkv_bias_terms.reshape(-1),
+            out_bias_grad,
+            gain_two_grad,
+            shift_two_grad,
+            up_bias_terms.reshape(-1),
+            down_bias_grad,
+        ),
+        AXES,
+    )
+    rms_stats = jnp.sqrt(totals[:3] / (totals[3] * width))
+    return (
+        layer_output[None],
+        input_grad[None],
+        gain_one_total,
+        shift_one_total,
+        qkv_out,
+        qkv_bias_total,
+        out_out,
+        out_bias_total,
+        gain_two_total,
+        shift_two_total,
+        up_out,
+        up_bias_total,
+        down_out,
+        down_bias_total,
+        rms_stats,
+    )
+
+
+def plane_program(mesh):
+    fine = Mesh(mesh.devices.reshape(2, 2, 4, 2), AXES)
+    dp, seq, both = ("y", "core"), ("z", "x"), AXES
+    return jax.shard_map(
+        plane_local,
+        mesh=fine,
+        in_specs=(
+            P(dp, seq, None),
+            P(dp, None),
+            P(dp),
+            P(dp),
+            P(both, None),
+            P(dp),
+            P(both, None),
+            P(dp),
+            P(dp),
+            P(dp),
+            P(dp, seq),
+            P(seq),
+            P(seq, dp),
+            P(dp),
+            P(dp, seq, None),
+        ),
+        out_specs=(
+            P(dp, seq, None),
+            P(dp, seq, None),
+            P(),
+            P(),
+            P(both, None),
+            P(),
+            P(both, None),
+            P(),
+            P(),
+            P(),
+            P(dp, seq),
+            P(),
+            P(seq, dp),
+            P(),
+            P(),
+        ),
+        check_vma=False,
+    )
+
+
 def solution(mesh):
+    if dict(mesh.shape) == {"dp": 4, "seq": 8}:
+        return plane_program(mesh)
     placed = (
         P("dp", "seq", None),
         P("dp", None),

time: 2200 us -> 1030 us (0.47)
  waiting for transfers between devices: 1700 us -> 386 us
  starting transfers between devices: 1.44 us -> 168 us
  matrix products: 253 us -> 128 us
  local copies, waits for them, and re-layouts: 22.8 us -> 117 us
  Pallas kernels: 0 us -> 39 us
    reduce_scatter x10 -> x4, waiting for transfers between devices: 936 us -> 61.8 us  [over_z(): lax.psum_scatter(value.astype(bf16), 'z', scatter_dimension=0, tiled=True)]
    all_gather x10 -> x4, waiting for transfers between devices: 764 us -> 4.71 us  [the longest x1 4.71 us: plane_local(): qkv_all = lax.all_gather(part, 'z', axis=0, tiled=True)]
    ppermute x0 -> x71, waiting for transfers between devices: none -> 167 us  [the longest x66 167 us: trade(): return lax.ppermute(value, axis, SWAP)]
    ppermute x0 -> x71, starting transfers between devices: none -> 140 us  [the longest x66 117 us: trade(): return lax.ppermute(value, axis, SWAP)]
    dot_general x18 -> x12, matrix products: 253 us -> 128 us  [matmul(): return jnp.einsum(how, left, right, preferred_element_type=jnp.float32)]
    psum x0 -> x1, waiting for transfers between devices: none -> 114 us  [plane_local(): lax.psum((square_sums, gain_one_grad, shift_one_grad, qkv_bias_terms.resh...]
    unnamed x126 -> x201, local copies, waits for them, and re-layouts: 13.4 us -> 55.1 us
    psum x1 -> x0, blocking collectives: 41.7 us -> none  [local(): lax.psum((square_sums, counted, gain_one_grad, shift_one_grad, qkv_bias_g...]
  transfers between devices with their start and end apart: 20 -> 86, of which waited for: 20 -> 33; matrix products, arithmetic and copies ran while one was open for 13% -> 28% of each run, Pallas kernels for 0% -> 4%
where the time goes in v1:
time: 1030 us; the launch traced here: 1020 us
  waiting for transfers between devices  386 us (37%)
  starting transfers between devices  168 us (16%)
  matrix products  128 us (12%)
  local copies, waits for them, and re-layouts  117 us (11%)
  other arithmetic  96.1 us (9%)
  blocking collectives  72 us (7%)
  Pallas kernels  39 us (4%)
  between operations  17.3 us (2%)
    ppermute x66, waiting for transfers between devices, trade(): return lax.ppermute(value, axis, SWAP)  167 us
    dot_general x12, matrix products, matmul(): return jnp.einsum(how, left, right, preferred_element_type=jnp.float32)  128 us
    ppermute x66, starting transfers between devices, trade(): return lax.ppermute(value, axis, SWAP)  117 us
    psum x1, waiting for transfers between devices, plane_local(): lax.psum((square_sums, gain_one_grad, shift_one_grad, qkv_bias_terms.resh...  114 us
    all_gather x1, blocking collectives, plane_local(): small = lax.all_gather(small, ('y', 'core', 'z'), axis=0, tiled=False)  72 us
    reduce_scatter x4, waiting for transfers between devices, over_z(): lax.psum_scatter(value.astype(bf16), 'z', scatter_dimension=0, tiled=True)  61.8 us
    unnamed x201, local copies, waits for them, and re-layouts  55.1 us
    all_to_all x1, waiting for transfers between devices, plane_local(): lax.all_to_all(w_down.reshape(4, quarter, -1), ('y', 'core'), 0, 0, tiled...  24 us
  transfers between devices with their start and end apart: 86, of which 33 were waited for; matrix products, arithmetic and copies ran while one was open for 28% of the time, Pallas kernels for 4%

profile of v1, /device:TPU:0, one launch (start us, length us, event | category | flops | bytes accessed | tf_op | source)
XLA Modules:
  0.0 1024.2 jit_solution(5935618679503324183)
XLA Ops:
  12.7 7.6 all-to-all-start
  23.6 72.0 %all-gather.2 = bf16[16,1,5632]{2,1,0:T(2,128)(2,1)S(1)} all-gather(bf16[1,1,5632]{2,1,0:T(2,128)(2,1)S(1)} %reshape.585), channel_id=2, replica_groups=mesh['y'=2,'core'=2,'z'=4,'x'=2] {'y','core','z'}, dimensions={0}, use_global_device_ids=true | all-gather | bytes 191488 | tf_op jit(solution)/shard_map/all_gather | solution.py:706
  102.2 2.9 multiply_cosine_fusion.1
  105.1 4.2 all-to-all-start.1
  120.3 26.0 %collective-permute-done.3 = bf16[256,2048]{1,0:T(8,128)(2,1)} collective-permute-done((bf16[256,2048]{1,0:T(8,128)(2,1)}, bf16[256,2048]{1,0:T(8,128)(2,1)}, u32[]{:S(2)}, u32[]{:S(2)}) %collective-permute-start.3) | collective-permute-done | bytes 1048608 | tf_op jit(solution)/shard_map/ppermute | solution.py:360
  156.8 5.4 collective-permute-done.7
  170.6 4.7 all-gather.8.cloned.1.call-done
  177.6 10.2 broadcast_add_fusion
  191.4 5.4 copy.116
  196.9 6.0 add_convert_fusion
  202.9 2.9 copy.117
  207.2 16.5 %attend.1 = (bf16[2048,256]{1,0:T(8,128)(2,1)S(1)}, f32[8,2,256]{2,1,0:T(2,128)S(1)}) custom-call(s32[8]{0:T(128)S(1)} %select_reduce_fusion.3.slot_of, s32[8]{0:T(128)S(1)} %and_select_fusion.first_of, bf16[2048,768]{1,0:T(8,128)(2,1)S(1)} %pad_maximum_fusion.qkv_ref, s32[8,1,256]{2,1,0:T(1,128)S(1)} %reduce_window_max.25.begin_ref), custom_call_target="tpu_custom_call" | custom-call | flops 3221225472 | bytes 5242880 | tf_op jit(solution)/shard_map/attend/pallas_call | solution.py:583
  226.1 3.3 copy-done.14
  235.5 4.1 collective-permute-done.12
  239.6 6.0 fusion.10
  251.9 12.3 %collective-permute-start.37 = (bf16[256,2048]{1,0:T(8,128)(2,1)S(1)}, bf16[256,2048]{1,0:T(8,128)(2,1)}, u32[]{:S(2)}, u32[]{:S(2)}) collective-permute-start(bf16[256,2048]{1,0:T(8,128)(2,1)S(1)} %collective-permute-done.36), channel_id=1, source_target_pairs={{0,8},{8,0},{1,9},{9,1},{2,10},{10,2},{3,11},{11,3},{4,12},{12,4},... | collective-permute-start | bytes 3145736 | tf_op jit(solution)/shard_map/ppermute | solution.py:360
  264.1 54.4 %collective-permute-start.38 = (bf16[256,2048]{1,0:T(8,128)(2,1)S(1)}, bf16[256,2048]{1,0:T(8,128)(2,1)}, u32[]{:S(2)}, u32[]{:S(2)}) collective-permute-start(bf16[256,2048]{1,0:T(8,128)(2,1)S(1)} %collective-permute-done.36), channel_id=1, source_target_pairs={{0,16},{16,0},{1,17},{17,1},{2,18},{18,2},{3,19},{19,3},{4,20},{20... | collective-permute-start | bytes 3145736 | tf_op jit(solution)/shard_map/ppermute | solution.py:360
  318.5 3.5 all-to-all-start.2
  324.9 3.0 fusion.35
  329.8 24.0 %all-to-all-done.2 = bf16[4,256,512]{2,1,0:T(8,128)(2,1)S(1)} async-done(((bf16[4,256,512]{2,1,0:T(8,128)(2,1)}), bf16[4,256,512]{2,1,0:T(8,128)(2,1)S(1)}, u32[]{:S(2)}, u32[]{:S(2)}) %all-to-all-start.2) | async-done | bytes 1048608 | tf_op jit(solution)/shard_map/all_to_all | solution.py:699
  366.5 9.8 collective-permute-done.18
  384.0 3.5 collective-permute-done.43
  391.0 18.8 %collective-permute-done.20 = bf16[256,2048]{1,0:T(8,128)(2,1)S(1)} collective-permute-done((bf16[256,2048]{1,0:T(8,128)(2,1)S(1)}, bf16[256,2048]{1,0:T(8,128)(2,1)S(1)}, u32[]{:S(2)}, u32[]{:S(2)}) %collective-permute-start.20) | collective-permute-done | bytes 1048608 | tf_op jit(solution)/shard_map/ppermute | solution.py:360
  418.5 6.0 collective-permute-done.24
  433.7 14.6 %fusion.46 = f32[2048,1024]{1,0:T(8,128)} fusion(bf16[2048,2048]{1,0:T(8,128)(2,1)} %constant_dynamic-update-slice_fusion.10, bf16[2048,1024]{1,0:T(8,128)(2,1)} %all-gather.10.cloned.1.call-done), kind=kOutput, calls=%fused_computation.249 | convolution fusion | flops 8589934592 | bytes 20971520 | tf_op jit(solution)/shard_map/ab,bc->ac/dot_general | solution.py:649
  448.3 18.6 %convert_reduce_fusion = (f32[1024]{0:T(1024)S(1)}, bf16[2048,1024]{1,0:T(8,128)(2,1)S(1)}) fusion(f32[2048,1024]{1,0:T(8,128)} %fusion.46, f32[1024]{0:T(1024)S(1)} %bitcast.403, bf16[2048,2048]{1,0:T(8,128)(2,1)} %copy-done.35, bf16[1024,2048]{0,1:T(8,128)(2,1)} %all-gather.12.cloned.1.call-done), kind=kOutput, calls=%fused_computation.19 | convolution fusion | flops 8638168064 | bytes 25174016 | tf_op jit(solution)/shard_map/td,fd->tf/dot_general | solution.py:649
  466.9 9.6 convolution_convert_fusion.1
  479.5 3.7 fusion.36
  483.9 12.7 %convolution_convert_fusion.5 = bf16[2048,1024]{0,1:T(8,128)(2,1)} fusion(bf16[2048,2048]{1,0:T(8,128)(2,1)} %constant_dynamic-update-slice_fusion.10, bf16[2048,1024]{1,0:T(8,128)(2,1)S(1)} %get-tuple-element.85), kind=kOutput, calls=%fused_computation.36 | convolution fusion | flops 8592031744 | bytes 16777216 | tf_op jit(solution)/shard_map/td,tf->df/dot_general | solution.py:649
  496.6 6.2 copy.134
  502.9 5.4 fusion.8
  512.7 16.1 %convolution_convert_fusion.2 = bf16[2048,2048]{1,0:T(8,128)(2,1)S(1)} fusion(bf16[1024,2048]{0,1:T(8,128)(2,1)} %all-gather.12.cloned.1.call-done, f32[2048,1024]{1,0:T(8,128)} %fusion.46, f32[1024]{0:T(1024)S(1)} %bitcast.404), kind=kOutput, calls=%fused_computation.23 | convolution fusion | flops 8615100416 | bytes 20975616 | tf_op jit(solution)/shard_map/ab,bc->ac/dot_general | solution.py:649
  535.6 8.3 collective-permute-done.47
  543.9 9.9 collective-permute-done.49
  555.7 3.7 convert_reduce_fusion.4
  561.2 16.7 %convolution_convert_fusion.4 = bf16[1024,2048]{1,0:T(8,128)(2,1)} fusion(bf16[2048,2048]{1,0:T(8,128)(2,1)} %copy-done.35, f32[2048,1024]{1,0:T(8,128)} %fusion.46, f32[1024]{0:T(1024)S(1)} %bitcast.405), kind=kOutput, calls=%fused_computation.35 | convolution fusion | flops 8613003264 | bytes 20975616 | tf_op jit(solution)/shard_map/tf,td->fd/dot_general | solution.py:649
  578.0 7.3 collective-permute-done.54
  585.3 5.4 fusion.9
  598.2 8.5 collective-permute-done.58
  613.2 22.5 %attend_back.1 = bf16[2048,768]{1,0:T(8,128)(2,1)} custom-call(s32[8]{0:T(128)S(1)} %copy-done.6, s32[8]{0:T(128)S(1)} %copy-done.8, bf16[2048,768]{1,0:T(8,128)(2,1)} %copy-done.2, s32[8,1,256]{2,1,0:T(1,128)S(1)} %copy-done.4, f32[8,2,256]{2,1,0:T(2,128)S(1)} %get-tuple-element.18.lse_ref, bf16[2048,256]{1,0:T(8,128)(2,1)S(1)} %copy-done.1, ...), custom_call_target="tpu_custom_call" | custom-call | flops 8589934592 | bytes 12582912 | tf_op jit(solution)/shard_map/attend_back/pallas_call | solution.py:611
  635.7 8.9 convolution_convert_fusion
  651.9 12.4 %collective-permute-done.30 = bf16[128,2048]{1,0:T(8,128)(2,1)S(1)} collective-permute-done((bf16[128,2048]{1,0:T(8,128)(2,1)S(1)}, bf16[128,2048]{1,0:T(8,128)(2,1)S(1)}, u32[]{:S(2)}, u32[]{:S(2)}) %collective-permute-start.30) | collective-permute-done | bytes 524320 | tf_op jit(solution)/shard_map/ppermute | solution.py:360
  670.4 5.1 collective-permute-done.29
  675.5 4.1 collective-permute-done.31
  680.7 8.0 collective-permute-done.34
  691.2 5.9 convolution_convert_fusion.7
  698.3 4.1 fusion.7
  707.2 4.1 collective-permute-done.70
  714.8 7.7 collective-permute-done.64
  726.0 4.9 select_reduce_fusion.2
  730.9 3.2 pad_maximum_fusion.7
  739.8 6.0 collective-permute-done.68
  748.0 2.9 fusion.24
  751.0 10.2 convolution_convert_fusion.6
  763.3 4.3 all-to-all-start.4
  767.6 9.5 collective-permute-start.35
  782.1 4.3 all-to-all-start.5
  786.4 3.7 fusion.23
  790.2 9.5 collective-permute-start.69
  802.9 2.9 copy.137
  812.9 114.4 %all-reduce.3.cloned.1.call-done = (f32[2048]{0:T(1024)}, f32[2048]{0:T(1024)}, f32[6144]{0:T(1024)}, f32[2048]{0:T(1024)}, f32[2048]{0:T(1024)}, /*index=5*/f32...) async-done(((f32[2048]{0:T(1024)}, f32[2048]{0:T(1024)}, f32[6144]{0:T(1024)}, f32[2048]{0:T(1024)}, f32[2048]{0:T(1024)}, /*index=5*/f32[2048]{0:T(1024)}, ...) | async-done | bytes 106528 | tf_op jit(solution)/shard_map/psum | solution.py:838
  929.2 61.7 %reduce-scatter.5.cloned.1.call-done = bf16[512,768]{1,0:T(8,128)(2,1)} async-done(((bf16[2048,768]{1,0:T(8,128)(2,1)}), bf16[512,768]{1,0:T(8,128)(2,1)}) %reduce-scatter.5.cloned.1.call-update) | async-done | bytes 786448 | tf_op jit(solution)/shard_map/reduce_scatter | solution.py:799
  990.9 3.7 all-to-all-start.3
  998.5 8.1 all-to-all-done.3
  (467 shorter events, 215.7 us)
Async XLA Ops:
  7.3 102.9 %collective-permute-start = (bf16[256,2048]{1,0:T(8,128)(2,1)}, bf16[256,2048]{1,0:T(8,128)(2,1)S(1)}, u32[]{:S(2)}, u32[]{:S(2)}) collective-permute-start(bf16[256,2048]{1,0:T(8,128)(2,1)} %bitcast.408), channel_id=1, source_target_pairs={{0,0},{1,1},{2,16},{3,17},{4,24},{5,25},{6,8},{7,9},{8,6},{9,7},{1... | collective-permute-start | bytes 3145736 | tf_op jit(solution)/shard_map/ppermute | solution.py:369
  12.7 92.4 %all-to-all-start = ((bf16[8,64,768]{2,1,0:T(8,128)(2,1)}), bf16[8,64,768]{2,1,0:T(8,128)(2,1)S(1)}, u32[]{:S(2)}, u32[]{:S(2)}) async-start(bf16[8,64,768]{2,1,0:T(8,128)(2,1)} %all_to_all.26), calls=%async_computation | async-start | bytes 1572864 | tf_op jit(solution)/shard_map/all_to_all | solution.py:682
  20.3 94.8 %all-gather.14.cloned.1.call-start = ((), (), s32[]{:S(2)}) async-start(), calls=%async_computation.17 | async-start | bytes 1310720 | tf_op jit(solution)/shard_map/all_gather | solution.py:687
  20.3 78.7 %collective-permute-start.1 = (s32[1,2048]{1,0:T(1,128)S(1)}, s32[1,2048]{1,0:T(1,128)S(1)}, u32[]{:S(2)}, u32[]{:S(2)}) collective-permute-start(s32[1,2048]{1,0:T(1,128)S(1)} %copy-done.64), channel_id=1, source_target_pairs={{0,0},{1,1},{2,16},{3,17},{4,24},{5,25},{6,8},{7,9},{8,6},{9,7},{1... | collective-permute-start | bytes 24584 | tf_op jit(solution)/shard_map/ppermute | solution.py:369
  105.1 127.0 %all-to-all-start.1 = ((bf16[4,512,256]{1,2,0:T(8,128)(2,1)}), bf16[4,512,256]{1,2,0:T(8,128)(2,1)}, u32[]{:S(2)}, u32[]{:S(2)}) async-start(bf16[4,512,256]{1,2,0:T(8,128)(2,1)} %bitcast.32), calls=%async_computation.1 | async-start | bytes 2097152 | tf_op jit(solution)/shard_map/all_to_all | solution.py:697
  109.4 66.0 %all-gather.8.cloned.1.call-start = ((), (), s32[]{:S(2)}) async-start(), calls=%async_computation.10 | async-start | bytes 3932160 | tf_op jit(solution)/shard_map/all_gather | solution.py:683
  110.1 323.6 %all-gather.10.cloned.1.call-start = ((), (), s32[]{:S(2)}) async-start(), calls=%async_computation.11 | async-start | bytes 5242880 | tf_op jit(solution)/shard_map/all_gather | solution.py:698
  112.7 33.7 %collective-permute-start.3 = (bf16[256,2048]{1,0:T(8,128)(2,1)}, bf16[256,2048]{1,0:T(8,128)(2,1)}, u32[]{:S(2)}, u32[]{:S(2)}) collective-permute-start(bf16[256,2048]{1,0:T(8,128)(2,1)} %get-tuple-element.96), channel_id=1, source_target_pairs={{0,16},{16,0},{1,17},{17,1},{2,18},{18,2},{3,19},{19,3},{4,20},{20... | collective-permute-start | bytes 3145736 | tf_op jit(solution)/shard_map/ppermute | solution.py:360
  114.7 33.2 %collective-permute-start.5 = (bf16[256,2048]{1,0:T(8,128)(2,1)}, bf16[256,2048]{1,0:T(8,128)(2,1)}, u32[]{:S(2)}, u32[]{:S(2)}) collective-permute-start(bf16[256,2048]{1,0:T(8,128)(2,1)} %get-tuple-element.96), channel_id=1, source_target_pairs={{0,1},{1,0},{2,3},{3,2},{4,5},{5,4},{6,7},{7,6},{8,9},{9,8},{10,11... | collective-permute-start | bytes 3145736 | tf_op jit(solution)/shard_map/ppermute | solution.py:360
  116.4 35.9 %collective-permute-start.11 = (bf16[2,64,2048]{2,1,0:T(8,128)(2,1)S(1)}, bf16[2,64,2048]{2,1,0:T(8,128)(2,1)S(1)}, u32[]{:S(2)}, u32[]{:S(2)}) collective-permute-start(bf16[2,64,2048]{2,1,0:T(8,128)(2,1)S(1)} %bitcast.379), channel_id=1, source_target_pairs={{0,1},{1,0},{2,3},{3,2},{4,5},{5,4},{6,7},{7,6},{8,9},{9,8},{10,11... | collective-permute-start | bytes 1572872 | tf_op jit(solution)/shard_map/ppermute | solution.py:360
  118.3 35.1 %collective-permute-start.2 = (bf16[256,2048]{1,0:T(8,128)(2,1)}, bf16[256,2048]{1,0:T(8,128)(2,1)S(1)}, u32[]{:S(2)}, u32[]{:S(2)}) collective-permute-start(bf16[256,2048]{1,0:T(8,128)(2,1)} %get-tuple-element.96), channel_id=1, source_target_pairs={{0,8},{8,0},{1,9},{9,1},{2,10},{10,2},{3,11},{11,3},{4,12},{12,4},... | collective-permute-start | bytes 3145736 | tf_op jit(solution)/shard_map/ppermute | solution.py:360
  147.4 14.8 %collective-permute-start.7 = (bf16[128,2048]{1,0:T(8,128)(2,1)S(1)}, bf16[128,2048]{1,0:T(8,128)(2,1)S(1)}, u32[]{:S(2)}, u32[]{:S(2)}) collective-permute-start(bf16[128,2048]{1,0:T(8,128)(2,1)S(1)} %slice.275), channel_id=1, source_target_pairs={{0,1},{1,0},{2,3},{3,2},{4,5},{5,4},{6,7},{7,6},{8,9},{9,8},{10,11... | collective-permute-start | bytes 1572872 | tf_op jit(solution)/shard_map/ppermute | solution.py:360
  234.4 17.5 %collective-permute-start.36 = (bf16[256,2048]{1,0:T(8,128)(2,1)S(1)}, bf16[256,2048]{1,0:T(8,128)(2,1)S(1)}, u32[]{:S(2)}, u32[]{:S(2)}) collective-permute-start(bf16[256,2048]{1,0:T(8,128)(2,1)S(1)} %bitcast.409), channel_id=1, source_target_pairs={{0,0},{1,1},{2,16},{3,17},{4,24},{5,25},{6,8},{7,9},{8,6},{9,7},{1... | collective-permute-start | bytes 3145736 | tf_op jit(solution)/shard_map/ppermute | solution.py:369
  249.0 75.3 %collective-permute-start.14 = (bf16[128,2048]{1,0:T(8,128)(2,1)}, bf16[128,2048]{1,0:T(8,128)(2,1)}, u32[]{:S(2)}, u32[]{:S(2)}) collective-permute-start(bf16[128,2048]{1,0:T(8,128)(2,1)} %get-tuple-element.119), channel_id=1, source_target_pairs={{0,1},{1,0},{2,3},{3,2},{4,5},{5,4},{6,7},{7,6},{8,9},{9,8},{10,11... | collective-permute-start | bytes 1572872 | tf_op jit(solution)/shard_map/ppermute | solution.py:360
  250.4 74.5 %collective-permute-start.16 = (bf16[128,2048]{1,0:T(8,128)(2,1)}, bf16[128,2048]{1,0:T(8,128)(2,1)}, u32[]{:S(2)}, u32[]{:S(2)}) collective-permute-start(bf16[128,2048]{1,0:T(8,128)(2,1)} %get-tuple-element.118), channel_id=1, source_target_pairs={{0,16},{16,0},{1,17},{17,1},{2,18},{18,2},{3,19},{19,3},{4,20},{20... | collective-permute-start | bytes 1572872 | tf_op jit(solution)/shard_map/ppermute | solution.py:360
  251.9 103.4 %collective-permute-start.37 = (bf16[256,2048]{1,0:T(8,128)(2,1)S(1)}, bf16[256,2048]{1,0:T(8,128)(2,1)}, u32[]{:S(2)}, u32[]{:S(2)}) collective-permute-start(bf16[256,2048]{1,0:T(8,128)(2,1)S(1)} %collective-permute-done.36), channel_id=1, source_target_pairs={{0,8},{8,0},{1,9},{9,1},{2,10},{10,2},{3,11},{11,3},{4,12},{12,4},... | collective-permute-start | bytes 3145736 | tf_op jit(solution)/shard_map/ppermute | solution.py:360
  264.1 93.2 %collective-permute-start.38 = (bf16[256,2048]{1,0:T(8,128)(2,1)S(1)}, bf16[256,2048]{1,0:T(8,128)(2,1)}, u32[]{:S(2)}, u32[]{:S(2)}) collective-permute-start(bf16[256,2048]{1,0:T(8,128)(2,1)S(1)} %collective-permute-done.36), channel_id=1, source_target_pairs={{0,16},{16,0},{1,17},{17,1},{2,18},{18,2},{3,19},{19,3},{4,20},{20... | collective-permute-start | bytes 3145736 | tf_op jit(solution)/shard_map/ppermute | solution.py:360
  318.5 35.2 %all-to-all-start.2 = ((bf16[4,256,512]{2,1,0:T(8,128)(2,1)}), bf16[4,256,512]{2,1,0:T(8,128)(2,1)S(1)}, u32[]{:S(2)}, u32[]{:S(2)}) async-start(bf16[4,256,512]{2,1,0:T(8,128)(2,1)} %bitcast.374), calls=%async_computation.2 | async-start | bytes 2097152 | tf_op jit(solution)/shard_map/all_to_all | solution.py:699
  322.1 126.2 %all-gather.12.cloned.1.call-start = ((), (), s32[]{:S(2)}) async-start(), calls=%async_computation.12 | async-start | bytes 5242880 | tf_op jit(solution)/shard_map/all_gather | solution.py:703
  322.8 38.4 %collective-permute-start.40 = (bf16[256,2048]{1,0:T(8,128)(2,1)S(1)}, bf16[256,2048]{1,0:T(8,128)(2,1)}, u32[]{:S(2)}, u32[]{:S(2)}) collective-permute-start(bf16[256,2048]{1,0:T(8,128)(2,1)S(1)} %collective-permute-done.36), channel_id=1, source_target_pairs={{0,1},{1,0},{2,3},{3,2},{4,5},{5,4},{6,7},{7,6},{8,9},{9,8},{10,11... | collective-permute-start | bytes 3145736 | tf_op jit(solution)/shard_map/ppermute | solution.py:360
  324.3 38.6 %collective-permute-start.13 = (bf16[128,2048]{1,0:T(8,128)(2,1)}, bf16[128,2048]{1,0:T(8,128)(2,1)}, u32[]{:S(2)}, u32[]{:S(2)}) collective-permute-start(bf16[128,2048]{1,0:T(8,128)(2,1)} %get-tuple-element.116), channel_id=1, source_target_pairs={{0,1},{1,0},{2,3},{3,2},{4,5},{5,4},{6,7},{7,6},{8,9},{9,8},{10,11... | collective-permute-start | bytes 1572872 | tf_op jit(solution)/shard_map/ppermute | solution.py:360
  327.8 37.3 %collective-permute-start.15 = (bf16[128,2048]{1,0:T(8,128)(2,1)}, bf16[128,2048]{1,0:T(8,128)(2,1)}, u32[]{:S(2)}, u32[]{:S(2)}) collective-permute-start(bf16[128,2048]{1,0:T(8,128)(2,1)} %get-tuple-element.120), channel_id=1, source_target_pairs={{0,16},{16,0},{1,17},{17,1},{2,18},{18,2},{3,19},{19,3},{4,20},{20... | collective-permute-start | bytes 1572872 | tf_op jit(solution)/shard_map/ppermute | solution.py:360
  355.1 408.2 %reduce-scatter.9.cloned.1.call-start = ((), (), s32[]{:S(2)}) async-start(), calls=%async_computation.15 | async-start | bytes 5242880 | tf_op jit(solution)/shard_map/reduce_scatter | solution.py:799
  355.3 21.0 %collective-permute-start.18 = (bf16[128,2048]{1,0:T(8,128)(2,1)}, bf16[128,2048]{1,0:T(8,128)(2,1)S(1)}, u32[]{:S(2)}, u32[]{:S(2)}) collective-permute-start(bf16[128,2048]{1,0:T(8,128)(2,1)} %get-tuple-element.117), channel_id=1, source_target_pairs={{0,16},{16,0},{1,17},{17,1},{2,18},{18,2},{3,19},{19,3},{4,20},{20... | collective-permute-start | bytes 1572872 | tf_op jit(solution)/shard_map/ppermute | solution.py:360
  357.3 19.0 %collective-permute-start.17 = (bf16[128,2048]{1,0:T(8,128)(2,1)}, bf16[128,2048]{1,0:T(8,128)(2,1)S(1)}, u32[]{:S(2)}, u32[]{:S(2)}) collective-permute-start(bf16[128,2048]{1,0:T(8,128)(2,1)} %get-tuple-element.121), channel_id=1, source_target_pairs={{0,1},{1,0},{2,3},{3,2},{4,5},{5,4},{6,7},{7,6},{8,9},{9,8},{10,11... | collective-permute-start | bytes 1572872 | tf_op jit(solution)/shard_map/ppermute | solution.py:360
  361.2 22.5 %collective-permute-start.42 = (bf16[128,2048]{1,0:T(8,128)(2,1)S(1)}, bf16[128,2048]{1,0:T(8,128)(2,1)S(1)}, u32[]{:S(2)}, u32[]{:S(2)}) collective-permute-start(bf16[128,2048]{1,0:T(8,128)(2,1)S(1)} %slice.307), channel_id=1, source_target_pairs={{0,1},{1,0},{2,3},{3,2},{4,5},{5,4},{6,7},{7,6},{8,9},{9,8},{10,11... | collective-permute-start | bytes 1572872 | tf_op jit(solution)/shard_map/ppermute | solution.py:360
  363.0 24.5 %collective-permute-start.43 = (bf16[128,2048]{1,0:T(8,128)(2,1)S(1)}, bf16[128,2048]{1,0:T(8,128)(2,1)S(1)}, u32[]{:S(2)}, u32[]{:S(2)}) collective-permute-start(bf16[128,2048]{1,0:T(8,128)(2,1)S(1)} %slice.308), channel_id=1, source_target_pairs={{0,16},{16,0},{1,17},{17,1},{2,18},{18,2},{3,19},{19,3},{4,20},{20... | collective-permute-start | bytes 1572872 | tf_op jit(solution)/shard_map/ppermute | solution.py:360
  365.1 22.4 %collective-permute-start.39 = (bf16[256,2048]{1,0:T(8,128)(2,1)}, bf16[256,2048]{1,0:T(8,128)(2,1)S(1)}, u32[]{:S(2)}, u32[]{:S(2)}) collective-permute-start(bf16[256,2048]{1,0:T(8,128)(2,1)} %collective-permute-done.38), channel_id=1, source_target_pairs={{0,8},{8,0},{1,9},{9,1},{2,10},{10,2},{3,11},{11,3},{4,12},{12,4},... | collective-permute-start | bytes 3145736 | tf_op jit(solution)/shard_map/ppermute | solution.py:360
  380.4 29.4 %collective-permute-start.20 = (bf16[256,2048]{1,0:T(8,128)(2,1)S(1)}, bf16[256,2048]{1,0:T(8,128)(2,1)S(1)}, u32[]{:S(2)}, u32[]{:S(2)}) collective-permute-start(bf16[256,2048]{1,0:T(8,128)(2,1)S(1)} %get-tuple-element.90), channel_id=1, source_target_pairs={{0,16},{16,0},{1,17},{17,1},{2,18},{18,2},{3,19},{19,3},{4,20},{20... | collective-permute-start | bytes 3145736 | tf_op jit(solution)/shard_map/ppermute | solution.py:360
  383.7 26.2 %collective-permute-start.44 = (bf16[128,2048]{1,0:T(8,128)(2,1)S(1)}, bf16[128,2048]{1,0:T(8,128)(2,1)S(1)}, u32[]{:S(2)}, u32[]{:S(2)}) collective-permute-start(bf16[128,2048]{1,0:T(8,128)(2,1)S(1)} %collective-permute-done.42), channel_id=1, source_target_pairs={{0,8},{8,0},{1,9},{9,1},{2,10},{10,2},{3,11},{11,3},{4,12},{12,4},... | collective-permute-start | bytes 1572872 | tf_op jit(solution)/shard_map/ppermute | solution.py:360
  387.5 28.1 %collective-permute-start.45 = (bf16[128,2048]{1,0:T(8,128)(2,1)S(1)}, bf16[128,2048]{1,0:T(8,128)(2,1)S(1)}, u32[]{:S(2)}, u32[]{:S(2)}) collective-permute-start(bf16[128,2048]{1,0:T(8,128)(2,1)S(1)} %collective-permute-done.43), channel_id=1, source_target_pairs={{0,8},{8,0},{1,9},{9,1},{2,10},{10,2},{3,11},{11,3},{4,12},{12,4},... | collective-permute-start | bytes 1572872 | tf_op jit(solution)/shard_map/ppermute | solution.py:360
  387.6 25.7 %collective-permute-start.22 = (bf16[256,2048]{1,0:T(8,128)(2,1)S(1)}, bf16[256,2048]{1,0:T(8,128)(2,1)S(1)}, u32[]{:S(2)}, u32[]{:S(2)}) collective-permute-start(bf16[256,2048]{1,0:T(8,128)(2,1)S(1)} %get-tuple-element.90), channel_id=1, source_target_pairs={{0,1},{1,0},{2,3},{3,2},{4,5},{5,4},{6,7},{7,6},{8,9},{9,8},{10,11... | collective-permute-start | bytes 3145736 | tf_op jit(solution)/shard_map/ppermute | solution.py:360
  390.5 25.1 %collective-permute-start.19 = (bf16[256,2048]{1,0:T(8,128)(2,1)S(1)}, bf16[256,2048]{1,0:T(8,128)(2,1)S(1)}, u32[]{:S(2)}, u32[]{:S(2)}) collective-permute-start(bf16[256,2048]{1,0:T(8,128)(2,1)S(1)} %get-tuple-element.90), channel_id=1, source_target_pairs={{0,8},{8,0},{1,9},{9,1},{2,10},{10,2},{3,11},{11,3},{4,12},{12,4},... | collective-permute-start | bytes 3145736 | tf_op jit(solution)/shard_map/ppermute | solution.py:360
  409.8 17.4 %collective-permute-start.21 = (bf16[256,2048]{1,0:T(8,128)(2,1)S(1)}, bf16[256,2048]{1,0:T(8,128)(2,1)S(1)}, u32[]{:S(2)}, u32[]{:S(2)}) collective-permute-start(bf16[256,2048]{1,0:T(8,128)(2,1)S(1)} %collective-permute-done.20), channel_id=1, source_target_pairs={{0,8},{8,0},{1,9},{9,1},{2,10},{10,2},{3,11},{11,3},{4,12},{12,4},... | collective-permute-start | bytes 3145736 | tf_op jit(solution)/shard_map/ppermute | solution.py:360
  479.0 23.8 %collective-permute-start.46 = (bf16[2,2,256,2048]{3,2,1,0:T(8,128)(2,1)}, bf16[2,2,256,2048]{3,2,1,0:T(8,128)(2,1)}, u32[]{:S(2)}, u32[]{:S(2)}) collective-permute-start(bf16[2,2,256,2048]{3,2,1,0:T(8,128)(2,1)} %slice_bitcast_fusion.2), channel_id=1, source_target_pairs={{0,8},{8,0},{1,9},{9,1},{2,10},{10,2},{3,11},{11,3},{4,12},{12,4},... | collective-permute-start | bytes 12582920 | tf_op jit(solution)/shard_map/ppermute | solution.py:360
  502.8 274.3 %reduce-scatter.11.cloned.1.call-start = ((), (), s32[]{:S(2)}) async-start(), calls=%async_computation.16 | async-start | bytes 5242880 | tf_op jit(solution)/shard_map/reduce_scatter | solution.py:799
  509.4 20.2 %collective-permute-start.48 = (bf16[128,2048]{1,0:T(8,128)(2,1)S(1)}, bf16[128,2048]{1,0:T(8,128)(2,1)S(1)}, u32[]{:S(2)}, u32[]{:S(2)}) collective-permute-start(bf16[128,2048]{1,0:T(8,128)(2,1)S(1)} %get-tuple-element.107), channel_id=1, source_target_pairs={{0,1},{1,0},{2,3},{3,2},{4,5},{5,4},{6,7},{7,6},{8,9},{9,8},{10,11... | collective-permute-start | bytes 1572872 | tf_op jit(solution)/shard_map/ppermute | solution.py:360
  510.9 18.7 %collective-permute-start.50 = (bf16[128,2048]{1,0:T(8,128)(2,1)S(1)}, bf16[128,2048]{1,0:T(8,128)(2,1)S(1)}, u32[]{:S(2)}, u32[]{:S(2)}) collective-permute-start(bf16[128,2048]{1,0:T(8,128)(2,1)S(1)} %get-tuple-element.106), channel_id=1, source_target_pairs={{0,16},{16,0},{1,17},{17,1},{2,18},{18,2},{3,19},{19,3},{4,20},{20... | collective-permute-start | bytes 1572872 | tf_op jit(solution)/shard_map/ppermute | solution.py:360
  528.7 15.1 %collective-permute-start.47 = (bf16[128,2048]{1,0:T(8,128)(2,1)}, bf16[128,2048]{1,0:T(8,128)(2,1)S(1)}, u32[]{:S(2)}, u32[]{:S(2)}) collective-permute-start(bf16[128,2048]{1,0:T(8,128)(2,1)} %get-tuple-element.104), channel_id=1, source_target_pairs={{0,1},{1,0},{2,3},{3,2},{4,5},{5,4},{6,7},{7,6},{8,9},{9,8},{10,11... | collective-permute-start | bytes 1572872 | tf_op jit(solution)/shard_map/ppermute | solution.py:360
  529.4 24.6 %collective-permute-start.52 = (bf16[128,2048]{1,0:T(8,128)(2,1)}, bf16[128,2048]{1,0:T(8,128)(2,1)S(1)}, u32[]{:S(2)}, u32[]{:S(2)}) collective-permute-start(bf16[128,2048]{1,0:T(8,128)(2,1)} %get-tuple-element.105), channel_id=1, source_target_pairs={{0,16},{16,0},{1,17},{17,1},{2,18},{18,2},{3,19},{19,3},{4,20},{20... | collective-permute-start | bytes 1572872 | tf_op jit(solution)/shard_map/ppermute | solution.py:360
  530.0 23.8 %collective-permute-start.49 = (bf16[128,2048]{1,0:T(8,128)(2,1)S(1)}, bf16[128,2048]{1,0:T(8,128)(2,1)S(1)}, u32[]{:S(2)}, u32[]{:S(2)}) collective-permute-start(bf16[128,2048]{1,0:T(8,128)(2,1)S(1)} %get-tuple-element.108), channel_id=1, source_target_pairs={{0,16},{16,0},{1,17},{17,1},{2,18},{18,2},{3,19},{19,3},{4,20},{20... | collective-permute-start | bytes 1572872 | tf_op jit(solution)/shard_map/ppermute | solution.py:360
  531.9 22.1 %collective-permute-start.51 = (bf16[128,2048]{1,0:T(8,128)(2,1)S(1)}, bf16[128,2048]{1,0:T(8,128)(2,1)S(1)}, u32[]{:S(2)}, u32[]{:S(2)}) collective-permute-start(bf16[128,2048]{1,0:T(8,128)(2,1)S(1)} %get-tuple-element.109), channel_id=1, source_target_pairs={{0,1},{1,0},{2,3},{3,2},{4,5},{5,4},{6,7},{7,6},{8,9},{9,8},{10,11... | collective-permute-start | bytes 1572872 | tf_op jit(solution)/shard_map/ppermute | solution.py:360
  535.6 49.7 %collective-permute-start.28 = (bf16[2,2,256,2048]{3,2,1,0:T(8,128)(2,1)}, bf16[2,2,256,2048]{3,2,1,0:T(8,128)(2,1)}, u32[]{:S(2)}, u32[]{:S(2)}) collective-permute-start(bf16[2,2,256,2048]{3,2,1,0:T(8,128)(2,1)} %slice_bitcast_fusion.4), channel_id=1, source_target_pairs={{0,8},{8,0},{1,9},{9,1},{2,10},{10,2},{3,11},{11,3},{4,12},{12,4},... | collective-permute-start | bytes 12582920 | tf_op jit(solution)/shard_map/ppermute | solution.py:360
  559.4 36.1 %collective-permute-start.53 = (bf16[256,2048]{1,0:T(8,128)(2,1)}, bf16[256,2048]{1,0:T(8,128)(2,1)}, u32[]{:S(2)}, u32[]{:S(2)}) collective-permute-start(bf16[256,2048]{1,0:T(8,128)(2,1)} %get-tuple-element.87), channel_id=1, source_target_pairs={{0,8},{8,0},{1,9},{9,1},{2,10},{10,2},{3,11},{11,3},{4,12},{12,4},... | collective-permute-start | bytes 3145736 | tf_op jit(solution)/shard_map/ppermute | solution.py:360
  559.4 25.9 %collective-permute-start.54 = (bf16[256,2048]{1,0:T(8,128)(2,1)}, bf16[256,2048]{1,0:T(8,128)(2,1)}, u32[]{:S(2)}, u32[]{:S(2)}) collective-permute-start(bf16[256,2048]{1,0:T(8,128)(2,1)} %get-tuple-element.87), channel_id=1, source_target_pairs={{0,16},{16,0},{1,17},{17,1},{2,18},{18,2},{3,19},{19,3},{4,20},{20... | collective-permute-start | bytes 3145736 | tf_op jit(solution)/shard_map/ppermute | solution.py:360
  559.8 34.0 %collective-permute-start.56 = (bf16[256,2048]{1,0:T(8,128)(2,1)}, bf16[256,2048]{1,0:T(8,128)(2,1)S(1)}, u32[]{:S(2)}, u32[]{:S(2)}) collective-permute-start(bf16[256,2048]{1,0:T(8,128)(2,1)} %get-tuple-element.87), channel_id=1, source_target_pairs={{0,1},{1,0},{2,3},{3,2},{4,5},{5,4},{6,7},{7,6},{8,9},{9,8},{10,11... | collective-permute-start | bytes 3145736 | tf_op jit(solution)/shard_map/ppermute | solution.py:360
  577.9 233.3 %reduce-scatter.7.cloned.1.call-start = ((), (), s32[]{:S(2)}) async-start(), calls=%async_computation.14 | async-start | bytes 1310720 | tf_op jit(solution)/shard_map/reduce_scatter | solution.py:799
  585.3 22.6 %collective-permute-start.55 = (bf16[256,2048]{1,0:T(8,128)(2,1)}, bf16[256,2048]{1,0:T(8,128)(2,1)S(1)}, u32[]{:S(2)}, u32[]{:S(2)}) collective-permute-start(bf16[256,2048]{1,0:T(8,128)(2,1)} %collective-permute-done.54), channel_id=1, source_target_pairs={{0,8},{8,0},{1,9},{9,1},{2,10},{10,2},{3,11},{11,3},{4,12},{12,4},... | collective-permute-start | bytes 3145736 | tf_op jit(solution)/shard_map/ppermute | solution.py:360
  647.1 51.2 %collective-permute-start.62 = (bf16[2,2,256,2048]{3,2,1,0:T(8,128)(2,1)}, bf16[2,2,256,2048]{3,2,1,0:T(8,128)(2,1)}, u32[]{:S(2)}, u32[]{:S(2)}) collective-permute-start(bf16[2,2,256,2048]{3,2,1,0:T(8,128)(2,1)} %slice_bitcast_fusion), channel_id=1, source_target_pairs={{0,8},{8,0},{1,9},{9,1},{2,10},{10,2},{3,11},{11,3},{4,12},{12,4},... | collective-permute-start | bytes 12582920 | tf_op jit(solution)/shard_map/ppermute | solution.py:360
  649.5 14.8 %collective-permute-start.30 = (bf16[128,2048]{1,0:T(8,128)(2,1)S(1)}, bf16[128,2048]{1,0:T(8,128)(2,1)S(1)}, u32[]{:S(2)}, u32[]{:S(2)}) collective-permute-start(bf16[128,2048]{1,0:T(8,128)(2,1)S(1)} %get-tuple-element.113), channel_id=1, source_target_pairs={{0,1},{1,0},{2,3},{3,2},{4,5},{5,4},{6,7},{7,6},{8,9},{9,8},{10,11... | collective-permute-start | bytes 1572872 | tf_op jit(solution)/shard_map/ppermute | solution.py:360
  650.8 24.7 %collective-permute-start.29 = (bf16[128,2048]{1,0:T(8,128)(2,1)}, bf16[128,2048]{1,0:T(8,128)(2,1)S(1)}, u32[]{:S(2)}, u32[]{:S(2)}) collective-permute-start(bf16[128,2048]{1,0:T(8,128)(2,1)} %get-tuple-element.110), channel_id=1, source_target_pairs={{0,1},{1,0},{2,3},{3,2},{4,5},{5,4},{6,7},{7,6},{8,9},{9,8},{10,11... | collective-permute-start | bytes 1572872 | tf_op jit(solution)/shard_map/ppermute | solution.py:360
  664.7 14.9 %collective-permute-start.31 = (bf16[128,2048]{1,0:T(8,128)(2,1)S(1)}, bf16[128,2048]{1,0:T(8,128)(2,1)S(1)}, u32[]{:S(2)}, u32[]{:S(2)}) collective-permute-start(bf16[128,2048]{1,0:T(8,128)(2,1)S(1)} %get-tuple-element.114), channel_id=1, source_target_pairs={{0,16},{16,0},{1,17},{17,1},{2,18},{18,2},{3,19},{19,3},{4,20},{20... | collective-permute-start | bytes 1572872 | tf_op jit(solution)/shard_map/ppermute | solution.py:360
  666.5 22.2 %collective-permute-start.34 = (bf16[128,2048]{1,0:T(8,128)(2,1)}, bf16[128,2048]{1,0:T(8,128)(2,1)}, u32[]{:S(2)}, u32[]{:S(2)}) collective-permute-start(bf16[128,2048]{1,0:T(8,128)(2,1)} %get-tuple-element.111), channel_id=1, source_target_pairs={{0,16},{16,0},{1,17},{17,1},{2,18},{18,2},{3,19},{19,3},{4,20},{20... | collective-permute-start | bytes 1572872 | tf_op jit(solution)/shard_map/ppermute | solution.py:360
  668.2 20.5 %collective-permute-start.33 = (bf16[128,2048]{1,0:T(8,128)(2,1)S(1)}, bf16[128,2048]{1,0:T(8,128)(2,1)}, u32[]{:S(2)}, u32[]{:S(2)}) collective-permute-start(bf16[128,2048]{1,0:T(8,128)(2,1)S(1)} %get-tuple-element.115), channel_id=1, source_target_pairs={{0,1},{1,0},{2,3},{3,2},{4,5},{5,4},{6,7},{7,6},{8,9},{9,8},{10,11... | collective-permute-start | bytes 1572872 | tf_op jit(solution)/shard_map/ppermute | solution.py:360
  705.8 16.7 %collective-permute-start.64 = (bf16[128,2048]{1,0:T(8,128)(2,1)}, bf16[128,2048]{1,0:T(8,128)(2,1)S(1)}, u32[]{:S(2)}, u32[]{:S(2)}) collective-permute-start(bf16[128,2048]{1,0:T(8,128)(2,1)} %get-tuple-element.101), channel_id=1, source_target_pairs={{0,1},{1,0},{2,3},{3,2},{4,5},{5,4},{6,7},{7,6},{8,9},{9,8},{10,11... | collective-permute-start | bytes 1572872 | tf_op jit(solution)/shard_map/ppermute | solution.py:360
  706.7 15.8 %collective-permute-start.66 = (bf16[128,2048]{1,0:T(8,128)(2,1)}, bf16[128,2048]{1,0:T(8,128)(2,1)S(1)}, u32[]{:S(2)}, u32[]{:S(2)}) collective-permute-start(bf16[128,2048]{1,0:T(8,128)(2,1)} %get-tuple-element.100), channel_id=1, source_target_pairs={{0,16},{16,0},{1,17},{17,1},{2,18},{18,2},{3,19},{19,3},{4,20},{20... | collective-permute-start | bytes 1572872 | tf_op jit(solution)/shard_map/ppermute | solution.py:360
  712.5 214.8 %all-reduce.3.cloned.1.call-start = ((), (), s32[]{:S(2)}) async-start(), calls=%async_computation.18 | async-start | bytes 214016 | tf_op jit(solution)/shard_map/psum | solution.py:838
  712.8 25.7 %collective-permute-start.63 = (bf16[128,2048]{1,0:T(8,128)(2,1)}, bf16[128,2048]{1,0:T(8,128)(2,1)}, u32[]{:S(2)}, u32[]{:S(2)}) collective-permute-start(bf16[128,2048]{1,0:T(8,128)(2,1)} %get-tuple-element.98), channel_id=1, source_target_pairs={{0,1},{1,0},{2,3},{3,2},{4,5},{5,4},{6,7},{7,6},{8,9},{9,8},{10,11... | collective-permute-start | bytes 1572872 | tf_op jit(solution)/shard_map/ppermute | solution.py:360
  750.9 240.0 %reduce-scatter.5.cloned.1.call-start = ((), (), s32[]{:S(2)}) async-start(), calls=%async_computation.13 | async-start | bytes 3932160 | tf_op jit(solution)/shard_map/reduce_scatter | solution.py:799
  763.3 18.8 %all-to-all-start.4 = ((bf16[4,512,256]{2,1,0:T(8,128)(2,1)}), bf16[4,512,256]{2,1,0:T(8,128)(2,1)}, u32[]{:S(2)}, u32[]{:S(2)}) async-start(bf16[4,512,256]{2,1,0:T(8,128)(2,1)} %bitcast.375), calls=%async_computation.7 | async-start | bytes 2097152 | tf_op jit(solution)/shard_map/all_to_all | solution.py:805
  767.6 32.1 %collective-permute-start.35 = (bf16[256,2048]{1,0:T(8,128)(2,1)}, bf16[256,2048]{1,0:T(8,128)(2,1)}, u32[]{:S(2)}, u32[]{:S(2)}) collective-permute-start(bf16[256,2048]{1,0:T(8,128)(2,1)} %get-tuple-element.97), channel_id=1, source_target_pairs={{0,0},{1,1},{2,16},{3,17},{4,24},{5,25},{6,8},{7,9},{8,6},{9,7},{1... | collective-permute-start | bytes 3145736 | tf_op jit(solution)/shard_map/ppermute | solution.py:369
  782.1 26.2 %all-to-all-start.5 = ((bf16[4,256,512]{2,1,0:T(8,128)(2,1)}), bf16[4,256,512]{2,1,0:T(8,128)(2,1)}, u32[]{:S(2)}, u32[]{:S(2)}) async-start(bf16[4,256,512]{2,1,0:T(8,128)(2,1)} %bitcast.363), calls=%async_computation.9 | async-start | bytes 2097152 | tf_op jit(solution)/shard_map/all_to_all | solution.py:802
  790.2 205.5 %collective-permute-start.69 = (bf16[256,2048]{1,0:T(8,128)(2,1)}, bf16[256,2048]{1,0:T(8,128)(2,1)}, u32[]{:S(2)}, u32[]{:S(2)}) collective-permute-start(bf16[256,2048]{1,0:T(8,128)(2,1)} %fusion.23), channel_id=1, source_target_pairs={{0,0},{1,1},{2,16},{3,17},{4,24},{5,25},{6,8},{7,9},{8,6},{9,7},{1... | collective-permute-start | bytes 3145736 | tf_op jit(solution)/shard_map/ppermute | solution.py:369
  990.9 15.8 %all-to-all-start.3 = ((bf16[8,64,768]{2,1,0:T(8,128)(2,1)}), bf16[8,64,768]{2,1,0:T(8,128)(2,1)S(1)}, u32[]{:S(2)}, u32[]{:S(2)}) async-start(bf16[8,64,768]{2,1,0:T(8,128)(2,1)} %bitcast.378), calls=%async_computation.4 | async-start | bytes 1572864 | tf_op jit(solution)/shard_map/all_to_all | solution.py:817
  (89 other events, 1888.6 us)
Sparse Core Ops, SparseCore 0:
  22.7 41.4 all-gather.13
  112.3 62.9 all-gather.7
  234.5 117.2 all-gather.9
  355.2 81.1 all-gather.11
  502.9 77.1 reduce-scatter.8
  582.4 77.2 reduce-scatter.10
  712.6 28.3 reduce-scatter.6
  751.0 176.2 all-reduce.2
  929.6 61.2 reduce-scatter.4
